TPU v7x, 32 devices: a whole 2x2x4 slice. The times are simulated.
32 devices in a mesh: row: 16 (over z, x, core), col: 1, chan: 2 (over y).
Axes of the slice: x: 2, y: 2, z: 4, core: 2. Of those that a mesh axis runs over, the one named last changes fastest.
Arguments:
- array_volts: bfloat16 [6, 2, 128, 2048], P('chan', None, ('row', 'col')), parts along dimension 0, may hold values from -15 to 15, as said below
- reference_volts: bfloat16 [6, 2, 32, 2048], P('chan', None, None, 'col'), parts along dimension 0, may hold values from -15 to 15, as said below
Outputs:
- cleaned: float32 [6, 2, 128, 128], P('chan', None, 'row', 'col'), parts along dimension 0
There are 2 independent parts, one for each index of `chan`. A program takes and returns all parts, laid end to end along the dimension named above; each array names one. Nothing has to cross between parts.
Inputs may be any that keep to these rules, and one draw needn't show every extreme that they name: `array_volts`: array voltages: common interference from a few sources plus independent noise. `reference_volts`: reference voltages: the same interference sources seen with other gains, plus independent noise.
All inputs are finite; a program needn't handle non-finite values.
Results may differ from a plain program's by a relative error of at most 0.0003.
Values may be sent and summed in bfloat16 or wider, within the bound.
No kernel may reach another device: no remote copies, remote signals or barrier semaphores. Data moves between devices by JAX's collectives and lax.ppermute only.
A program may use at most 64 MiB of HBM per device.

v0:
```python
import jax
import jax.numpy as jnp
from jax import lax
from jax.sharding import PartitionSpec as P


def correlate(first_rows, second_rows):
    width_first = first_rows.shape[1]
    width_second = second_rows.shape[1]
    samples = first_rows.shape[2]
    stacked_first = first_rows.reshape(2 * width_first, samples)
    stacked_second = second_rows.reshape(2 * width_second, samples)
    product = jnp.einsum(
        "xn,yn->xy", stacked_first, stacked_second, preferred_element_type=jnp.float32
    )
    real_part = product[:width_first, :width_second] + product[width_first:, width_second:]
    imaginary_portion = product[width_first:, :width_second] - product[:width_first, width_second:]
    return jnp.stack([real_part, imaginary_portion]) / jnp.float32(samples)


def conj_swap(cross_block):
    return jnp.stack([cross_block[0].T, -cross_block[1].T])


def subtract(vis_tile, rows_cross, cross_cols, reference_covariance):
    real_cov = reference_covariance[0]
    imag_cov = reference_covariance[1]
    system = jnp.concatenate(
        [jnp.concatenate([real_cov, -imag_cov], 1), jnp.concatenate([imag_cov, real_cov], 1)], 0
    )
    lower_factor = jnp.linalg.cholesky(system)
    right_hand = jnp.concatenate([cross_cols[0], cross_cols[1]], 0)
    middle = lax.linalg.triangular_solve(lower_factor, right_hand, left_side=True, lower=True)
    solved = lax.linalg.triangular_solve(
        lower_factor, middle, left_side=True, lower=True, transpose_a=True
    )
    half_size = real_cov.shape[0]
    solved_real = solved[:half_size]
    solved_imag = solved[half_size:]
    highest = lax.Precision.HIGHEST
    corr_real = jnp.dot(rows_cross[0], solved_real, precision=highest) - jnp.dot(
        rows_cross[1], solved_imag, precision=highest
    )
    corr_imag = jnp.dot(rows_cross[0], solved_imag, precision=highest) + jnp.dot(
        rows_cross[1], solved_real, precision=highest
    )
    return vis_tile - jnp.stack([corr_real, corr_imag])


def per_device(array_volts, reference_volts):
    results = []
    for sub_index in range(array_volts.shape[0]):
        local_volts = array_volts[sub_index]
        ref_all = lax.all_gather(reference_volts[sub_index], "col", axis=2, tiled=True)
        reference_covariance = correlate(ref_all, ref_all)
        own_cross = correlate(ref_all, local_volts)
        cross_row_block = lax.all_gather(own_cross, "col", axis=2, tiled=True)
        cross_cols = lax.all_gather(own_cross, "row", axis=2, tiled=True)
        rows_cross = conj_swap(cross_row_block)
        row_volts = lax.all_gather(local_volts, "col", axis=1, tiled=True)
        joined = correlate(row_volts, lax.all_gather(local_volts, "row", axis=1, tiled=True))
        results.append(subtract(joined, rows_cross, cross_cols, reference_covariance))
    return jnp.stack(results)


def solution(mesh):
    return jax.shard_map(
        per_device,
        mesh=mesh,
        in_specs=(P("chan", None, ("row", "col"), None), P("chan", None, None, "col")),
        out_specs=P("chan", None, "row", "col"),
        check_vma=False,
    )
```

profile of v0, /device:TPU:0, one launch (start us, length us, event | category | flops | bytes accessed | tf_op | source)
XLA Modules:
  0.0 138.5 jit_solution(9785705844547637499)
XLA Ops:
  6.5 1.6 %fusion.106 = (bf16[1,2,8,2048]{3,2,1,0:T(8,128)(2,1)}, bf16[1,2,8,2048]{3,2,1,0:T(8,128)(2,1)}, bf16[1,2,8,2048]{3,2,1,0:T(8,128)(2,1)}) fusion(bf16[3,2,8,2048]{3,2,1,0:T(8,128)(2,1)} %param.7), kind=kLoop, calls=%fused_computation.169 | loop fusion | bytes 393216 | tf_op jit(solution)/shard_map/slice | solution.py:53
  8.2 0.7 all-gather.11.cloned.1.call-update
  8.9 0.7 all-gather.9.cloned.1.call-update
  9.6 1.2 fusion.105
  12.8 5.9 %cholesky.70 = f32[64,64]{1,0:T(8,128)S(1)} custom-call(f32[64,64]{1,0:T(8,128)S(1)} %fusion.40), custom_call_target="Cholesky" | custom-call | tf_op jit(solution)/shard_map/jit(cholesky)/cholesky | solution.py:31
  18.7 0.6 compare_reduce_fusion.1
  19.3 0.7 fusion.31
  20.0 4.9 %custom-call.15 = f32[1,64,64]{1,2,0:T(8,128)S(1)} custom-call(f32[1,64,64]{2,1,0:T(8,128)S(1)} %fusion.31), custom_call_target="InvertDiagBlocksLowerTriangular" | custom-call | tf_op jit(solution)/shard_map/triangular_solve/custom-call.2 | solution.py:34
  24.9 23.6 %all_gather.30 = f32[2,32,128]{1,2,0:T(8,128)S(1)} all-gather(f32[2,32,8]{1,2,0:T(8,128)S(1)} %maximum_multiply_fusion.6), channel_id=1, replica_groups=mesh['row'=16,'col'=1,'chan'=2] {'row'}, dimensions={2}, use_global_device_ids=true | all-gather | bytes 34816 | tf_op jit(solution)/shard_map/all_gather | solution.py:58
  49.6 5.9 %cholesky.59 = f32[64,64]{1,0:T(8,128)S(1)} custom-call(f32[64,64]{1,0:T(8,128)S(1)} %fusion.44), custom_call_target="Cholesky" | custom-call | tf_op jit(solution)/shard_map/jit(cholesky)/cholesky | solution.py:31
  55.5 0.6 compare_reduce_fusion.2
  56.1 0.7 fusion.30
  56.8 4.9 %custom-call.13 = f32[1,64,64]{1,2,0:T(8,128)S(1)} custom-call(f32[1,64,64]{2,1,0:T(8,128)S(1)} %fusion.30), custom_call_target="InvertDiagBlocksLowerTriangular" | custom-call | tf_op jit(solution)/shard_map/triangular_solve/custom-call.2 | solution.py:34
  61.7 18.0 %all_gather.13 = f32[2,32,128]{1,2,0:T(8,128)S(1)} all-gather(f32[2,32,8]{1,2,0:T(8,128)S(1)} %maximum_multiply_fusion.4), channel_id=1, replica_groups=mesh['row'=16,'col'=1,'chan'=2] {'row'}, dimensions={2}, use_global_device_ids=true | all-gather | bytes 34816 | tf_op jit(solution)/shard_map/all_gather | solution.py:58
  80.7 5.9 %cholesky.81 = f32[64,64]{1,0:T(8,128)S(1)} custom-call(f32[64,64]{1,0:T(8,128)S(1)} %fusion.36), custom_call_target="Cholesky" | custom-call | tf_op jit(solution)/shard_map/jit(cholesky)/cholesky | solution.py:31
  86.6 0.6 compare_reduce_fusion
  87.3 0.7 fusion.32
  87.9 4.9 %custom-call.17 = f32[1,64,64]{1,2,0:T(8,128)S(1)} custom-call(f32[1,64,64]{2,1,0:T(8,128)S(1)} %fusion.32), custom_call_target="InvertDiagBlocksLowerTriangular" | custom-call | tf_op jit(solution)/shard_map/triangular_solve/custom-call.2 | solution.py:34
  93.2 19.3 %all_gather.32 = f32[2,32,128]{1,2,0:T(8,128)S(1)} all-gather(f32[2,32,8]{1,2,0:T(8,128)S(1)} %maximum_multiply_fusion.8), channel_id=1, replica_groups=mesh['row'=16,'col'=1,'chan'=2] {'row'}, dimensions={2}, use_global_device_ids=true | all-gather | bytes 34816 | tf_op jit(solution)/shard_map/all_gather | solution.py:58
  113.7 1.6 %fusion.28 = f32[16,256]{1,0:T(8,128)S(1)} fusion(bf16[256,2048]{1,0:T(8,128)(2,1)} %bitcast.183, bf16[3,2,8,2048]{3,2,1,0:T(8,128)(2,1)S(1)} %copy-done), kind=kOutput, calls=%fused_computation.40 | convolution fusion | flops 16777216 | bytes 1130496 | tf_op jit(solution)/shard_map/xn,yn->xy/dot_general | solution.py:13
  115.4 1.6 %fusion.20 = f32[16,256]{1,0:T(8,128)S(1)} fusion(bf16[256,2048]{1,0:T(8,128)(2,1)} %bitcast.184, bf16[3,2,8,2048]{3,2,1,0:T(8,128)(2,1)S(1)} %copy-done), kind=kOutput, calls=%fused_computation.32 | convolution fusion | flops 16777216 | bytes 1130496 | tf_op jit(solution)/shard_map/xn,yn->xy/dot_general | solution.py:13
  117.0 12.7 %all-gather.9.cloned.1.call-done = bf16[1,2,128,2048]{3,2,1,0:T(8,128)(2,1)} async-done(((bf16[1,2,8,2048]{3,2,1,0:T(8,128)(2,1)}), bf16[1,2,128,2048]{3,2,1,0:T(8,128)(2,1)}) %all-gather.9.cloned.1.call-update) | async-done | bytes 1048592 | tf_op jit(solution)/shard_map/all_gather | solution.py:61
  129.7 1.6 %fusion.24 = f32[16,256]{1,0:T(8,128)S(1)} fusion(bf16[256,2048]{1,0:T(8,128)(2,1)} %bitcast.185, bf16[3,2,8,2048]{3,2,1,0:T(8,128)(2,1)S(1)} %copy-done), kind=kOutput, calls=%fused_computation.36 | convolution fusion | flops 16777216 | bytes 1130496 | tf_op jit(solution)/shard_map/xn,yn->xy/dot_general | solution.py:13
  131.3 0.6 pad_maximum_fusion
  (70 shorter events, 5.8 us)
Async XLA Ops:
  6.5 107.2 %all-gather.7.cloned.1.call-start = ((), (), s32[]{:S(2)}) async-start(), calls=%async_computation | async-start | bytes 1114112 | tf_op jit(solution)/shard_map/all_gather | solution.py:61
  8.1 107.2 %all-gather.11.cloned.1.call-start = ((), (), s32[]{:S(2)}) async-start(), calls=%async_computation.2 | async-start | bytes 1114112 | tf_op jit(solution)/shard_map/all_gather | solution.py:61
  8.9 120.8 %all-gather.9.cloned.1.call-start = ((), (), s32[]{:S(2)}) async-start(), calls=%async_computation.1 | async-start | bytes 1114112 | tf_op jit(solution)/shard_map/all_gather | solution.py:61
  9.6 1.2 copy-start
Sparse Core Ops, SparseCore 0:
  9.5 41.2 all-gather.6
  53.0 37.3 all-gather.10
  92.6 36.9 all-gather.8
where the time goes:
time: 139 us; the launch traced here: 138 us
  blocking collectives  60.8 us (44%)
  other arithmetic  37.9 us (27%)
  waiting for transfers between devices  14.1 us (10%)
  between operations  13.4 us (10%)
  matrix products  9.02 us (6%)
  local copies, waits for them, and re-layouts  3.08 us (2%)
    all_gather x3, blocking collectives, per_device(): cross_cols = lax.all_gather(own_cross, 'row', axis=2, tiled=True)  60.8 us
    another operation x9, other arithmetic, subtract(): lower_factor = jnp.linalg.cholesky(system)  19.6 us
    another operation x6, other arithmetic, subtract(): lax.linalg.triangular_solve(lower_factor, middle, left_side=True, lower=T...  16.7 us
    all_gather x3, waiting for transfers between devices, per_device(): lax.all_gather(local_volts, 'row', axis=1, tiled=True)  12.7 us
    dot_general x9, matrix products, correlate(): jnp.einsum('xn,yn->xy', stacked_first, stacked_second, preferred_element_...  6.01 us
  transfers between devices with their start and end apart: 3, of which 1 were waited for; matrix products, arithmetic and copies ran while one was open for 33% of the time, Pallas kernels for 0%

commit v1 on v0

--- a/solution.py
+++ b/solution.py
@@ -1,7 +1,17 @@
+import functools
+
 import jax
 import jax.numpy as jnp
 from jax import lax
+from jax.experimental import pallas as pl
+from jax.experimental.pallas import tpu as pltpu
 from jax.sharding import PartitionSpec as P
+
+LANES = 128
+NT = (((1,), (1,)), ((), ()))
+TN = (((0,), (0,)), ((), ()))
+TT = (((0,), (1,)), ((), ()))
+HIGHEST = lax.Precision.HIGHEST
 
 
 def correlate(first_rows, second_rows):
@@ -37,17 +47,16 @@
     half_size = real_cov.shape[0]
     solved_real = solved[:half_size]
     solved_imag = solved[half_size:]
-    highest = lax.Precision.HIGHEST
-    corr_real = jnp.dot(rows_cross[0], solved_real, precision=highest) - jnp.dot(
-        rows_cross[1], solved_imag, precision=highest
-    )
-    corr_imag = jnp.dot(rows_cross[0], solved_imag, precision=highest) + jnp.dot(
-        rows_cross[1], solved_real, precision=highest
+    corr_real = jnp.dot(rows_cross[0], solved_real, precision=HIGHEST) - jnp.dot(
+        rows_cross[1], solved_imag, precision=HIGHEST
+    )
+    corr_imag = jnp.dot(rows_cross[0], solved_imag, precision=HIGHEST) + jnp.dot(
+        rows_cross[1], solved_real, precision=HIGHEST
     )
     return vis_tile - jnp.stack([corr_real, corr_imag])
 
 
-def per_device(array_volts, reference_volts):
+def per_device_any(array_volts, reference_volts):
     results = []
     for sub_index in range(array_volts.shape[0]):
         local_volts = array_volts[sub_index]
@@ -63,9 +72,190 @@
     return jnp.stack(results)
 
 
+def pack_body(volts_ref, reference_ref, message_ref, *, group):
+    subs, _, ants, samples = volts_ref.shape
+    members = message_ref.shape[0]
+    share = samples // group
+    tiles = share // LANES
+    base = subs * 2 * tiles * ants
+    for s in range(subs):
+        real, imag = volts_ref[s, 0], volts_ref[s, 1]
+        ref_real, ref_imag = reference_ref[s, 0], reference_ref[s, 1]
+        cross = lax.dot_general(
+            real, jnp.concatenate([ref_real, -ref_imag], 0), NT, preferred_element_type=jnp.float32
+        ) + lax.dot_general(
+            imag, jnp.concatenate([ref_imag, ref_real], 0), NT, preferred_element_type=jnp.float32
+        )
+        cross = cross / jnp.float32(samples)
+        high = cross.astype(jnp.bfloat16)
+        low = (cross - high.astype(jnp.float32)).astype(jnp.bfloat16)
+        both = jnp.concatenate([high, low], 1)
+        for m in range(members):
+            message_ref[m, base + s * ants : base + (s + 1) * ants, :] = both
+            for p in range(2):
+                for t in range(tiles):
+                    at = ((s * 2 + p) * tiles + t) * ants
+                    start = (m % group) * share + t * LANES
+                    message_ref[m, at : at + ants, :] = volts_ref[s, p, :, start : start + LANES]
+
+
+def solve_body(volts_ref, reference_ref, solved_ref):
+    subs, _, ants, samples = volts_ref.shape
+    nref = reference_ref.shape[2]
+    reals, imags = [], []
+    for s in range(subs):
+        real, imag = volts_ref[s, 0], volts_ref[s, 1]
+        ref_real, ref_imag = reference_ref[s, 0], reference_ref[s, 1]
+        first = jnp.concatenate([ref_real, real], 0)
+        second = jnp.concatenate([ref_imag, imag], 0)
+        dot = functools.partial(
+            lax.dot_general, dimension_numbers=NT, preferred_element_type=jnp.float32
+        )
+        reals.append((dot(ref_real, first) + dot(ref_imag, second)) / jnp.float32(samples))
+        imags.append((dot(ref_imag, first) - dot(ref_real, second)) / jnp.float32(samples))
+    re, im = jnp.stack(reals), jnp.stack(imags)
+    rows = lax.broadcasted_iota(jnp.int32, (1, nref, 1), 1)
+    for i in range(nref):
+        inverse = 1.0 / re[:, i : i + 1, i : i + 1]
+        row_re, row_im = re[:, i : i + 1, :] * inverse, im[:, i : i + 1, :] * inverse
+        col_re, col_im = re[:, :, i : i + 1], im[:, :, i : i + 1]
+        here = rows == i
+        re, im = (
+            jnp.where(here, row_re, re - (col_re * row_re - col_im * row_im)),
+            jnp.where(here, row_im, im - (col_re * row_im + col_im * row_re)),
+        )
+    solved_ref[:, 0] = re[:, :, nref:]
+    solved_ref[:, 1] = im[:, :, nref:]
+
+
+def joined(block):
+    members, ants, lanes = block.shape
+    return block.astype(jnp.float32).reshape(members * ants, lanes)
+
+
+def product_body(message_ref, partial_ref, *, group, subs, ants):
+    members = message_ref.shape[0]
+    rows = partial_ref.shape[1] // (subs * 2)
+    tiles = (message_ref.shape[1] // ants - subs) // (subs * 2)
+    mine = (lax.axis_index("row") // group) * group
+    for s in range(subs):
+        cols, own = [], []
+        for p in range(2):
+            for t in range(tiles):
+                at = ((s * 2 + p) * tiles + t) * ants
+                cols.append(joined(message_ref[:, at : at + ants, :]).astype(jnp.bfloat16))
+                own.append(joined(message_ref[pl.ds(mine, group), at : at + ants, :]))
+        right = jnp.concatenate(cols, 1)
+        upper = jnp.concatenate(own, 1)
+        lower = jnp.concatenate(own[tiles:] + [-x for x in own[:tiles]], 1)
+        left = jnp.concatenate([upper, lower], 0).astype(jnp.bfloat16)
+        out = lax.dot_general(left, right, NT, preferred_element_type=jnp.float32)
+        height = group * ants
+        for p in range(2):
+            at = (s * 2 + p) * rows
+            partial_ref[:, at : at + rows, :] = out[p * height : (p + 1) * height].reshape(
+                group, ants, members * ants
+            )
+
+
+def correction_body(message_ref, solved_ref, correction_ref):
+    subs, _, nref, ants = solved_ref.shape
+    base = message_ref.shape[1] - subs * ants
+    for s in range(subs):
+        cross = joined(message_ref[:, base + s * ants : base + (s + 1) * ants, :])
+        re, im = solved_ref[s, 0], solved_ref[s, 1]
+        for p, stack in enumerate(([re, -im], [-im, -re])):
+            column = jnp.concatenate(stack + stack, 0)
+            correction_ref[s, p] = lax.dot_general(
+                column, cross, TT, precision=HIGHEST, preferred_element_type=jnp.float32
+            )
+
+
+def finish_body(partial_ref, correction_ref, cleaned_ref, *, samples):
+    subs, _, ants, _ = cleaned_ref.shape
+    total = partial_ref[0]
+    for m in range(1, partial_ref.shape[0]):
+        total = total + partial_ref[m]
+    total = total / jnp.float32(samples)
+    for s in range(subs):
+        for p in range(2):
+            at = (s * 2 + p) * ants
+            cleaned_ref[s, p] = total[at : at + ants] - correction_ref[s, p]
+
+
+def call(body, out, *args, flops=0, moved=0, **kw):
+    spec = pl.BlockSpec(memory_space=pltpu.VMEM)
+    return pl.pallas_call(
+        functools.partial(body, **kw) if kw else body,
+        out_shape=out,
+        in_specs=[spec] * len(args),
+        out_specs=spec,
+        cost_estimate=pl.CostEstimate(flops=flops, bytes_accessed=moved, transcendentals=0),
+        name=body.__name__,
+    )(*args)
+
+
+def per_device(array_volts, reference_volts, *, n_row):
+    subs, _, ants, samples = array_volts.shape
+    nref = reference_volts.shape[2]
+    group = n_row // 2
+    tiles = samples // group // LANES
+    f32 = functools.partial(jax.ShapeDtypeStruct, dtype=jnp.float32)
+    height = subs * 2 * tiles * ants + subs * ants
+    message = call(
+        pack_body,
+        jax.ShapeDtypeStruct((n_row, height, LANES), jnp.bfloat16),
+        array_volts,
+        reference_volts,
+        group=group,
+    )
+    volts = lax.all_to_all(message, "row", split_axis=0, concat_axis=0, tiled=True)
+    solved = call(
+        solve_body,
+        f32((subs, 2, nref, ants)),
+        array_volts,
+        reference_volts,
+        flops=10**9,
+        moved=2 * 10**7,
+    )
+    partial = call(
+        product_body,
+        f32((group, subs * 2 * ants, n_row * ants)),
+        volts,
+        group=group,
+        subs=subs,
+        ants=ants,
+    )
+    groups = [list(range(group)), list(range(group, n_row))]
+    sums = lax.all_to_all(
+        partial, "row", split_axis=0, concat_axis=0, tiled=True, axis_index_groups=groups
+    )
+    correction = call(
+        correction_body,
+        f32((subs, 2, ants, n_row * ants)),
+        volts,
+        solved,
+        flops=10**8,
+        moved=2 * 10**6,
+    )
+    return call(
+        finish_body, f32((subs, 2, ants, n_row * ants)), sums, correction, samples=samples
+    )
+
+
 def solution(mesh):
+    n_row, n_col = mesh.shape["row"], mesh.shape["col"]
+
+    def body(array_volts, reference_volts):
+        samples = array_volts.shape[3]
+        nref = reference_volts.shape[2]
+        split = n_col == 1 and n_row % 2 == 0 and samples % (n_row // 2 * LANES) == 0
+        if split and 4 * nref == LANES:
+            return per_device(array_volts, reference_volts, n_row=n_row)
+        return per_device_any(array_volts, reference_volts)
+
     return jax.shard_map(
-        per_device,
+        body,
         mesh=mesh,
         in_specs=(P("chan", None, ("row", "col"), None), P("chan", None, None, "col")),
         out_specs=P("chan", None, "row", "col"),

time: 139 us -> 39.9 us (0.29)
  blocking collectives: 60.8 us -> 21.2 us
  other arithmetic: 37.9 us -> 0 us
  Pallas kernels: 0 us -> 14.2 us
  waiting for transfers between devices: 14.1 us -> 0.01 us
  between operations: 13.4 us -> 0.01 us
  matrix products: 9.02 us -> 0 us
  starting transfers between devices: 0.08 us -> 3.39 us
  local copies, waits for them, and re-layouts: 3.08 us -> 0.67 us
    all_gather x3 -> x0, blocking collectives: 60.8 us -> none  [per_device(): cross_cols = lax.all_gather(own_cross, 'row', axis=2, tiled=True)]
    another operation x25 -> x0, other arithmetic: 37.3 us -> none  [the longest x9 19.6 us: subtract(): lower_factor = jnp.linalg.cholesky(system)]
    all_to_all x0 -> x1, blocking collectives: none -> 21.2 us  [per_device(): lax.all_to_all(message, 'row', split_axis=0, concat_axis=0, tiled=True)]
    pallas_call x0 -> x5, Pallas kernels: none -> 14.2 us  [call(): pl.pallas_call(functools.partial(body, **kw) if kw else body, out_shape=o...]
    all_gather x3 -> x0, waiting for transfers between devices: 12.7 us -> none  [per_device(): lax.all_gather(local_volts, 'row', axis=1, tiled=True)]
    dot_general x21 -> x0, matrix products: 7.61 us -> none  [the longest x9 6.01 us: correlate(): jnp.einsum('xn,yn->xy', stacked_first, stacked_second, preferred_element_...]
    all_to_all x0 -> x1, starting transfers between devices: none -> 3.39 us  [per_device(): lax.all_to_all(partial, 'row', split_axis=0, concat_axis=0, tiled=True, a...]
    slice x2 -> x0, local copies, waits for them, and re-layouts: 2.8 us -> none  [the longest x1 1.59 us: per_device(): local_volts = array_volts[sub_index]]
  transfers between devices with their start and end apart: 3 -> 1, of which waited for: 1 -> 0; matrix products, arithmetic and copies ran while one was open for 33% -> 0% of each run, Pallas kernels for 0% -> 20%
where the time goes in v1:
time: 39.9 us; the launch traced here: 39.5 us
  blocking collectives  21.2 us (53%)
  Pallas kernels  14.2 us (36%)
  starting transfers between devices  3.39 us (8%)
  local copies, waits for them, and re-layouts  0.67 us (2%)
    all_to_all x1, blocking collectives, per_device(): lax.all_to_all(message, 'row', split_axis=0, concat_axis=0, tiled=True)  21.2 us
    pallas_call x5, Pallas kernels, call(): pl.pallas_call(functools.partial(body, **kw) if kw else body, out_shape=o...  14.2 us
    all_to_all x1, starting transfers between devices, per_device(): lax.all_to_all(partial, 'row', split_axis=0, concat_axis=0, tiled=True, a...  3.39 us
  transfers between devices with their start and end apart: 1, of which 0 were waited for; matrix products, arithmetic and copies ran while one was open for 0% of the time, Pallas kernels for 20%

profile of v1, /device:TPU:0, one launch (start us, length us, event | category | flops | bytes accessed | tf_op | source)
XLA Modules:
  0.0 39.5 jit_solution(808999321592422750)
XLA Ops:
  0.0 2.7 %pack_body.1 = bf16[16,120,128]{2,1,0:T(8,128)(2,1)} custom-call(bf16[3,2,8,2048]{3,2,1,0:T(8,128)(2,1)} %volts_ref.3, bf16[3,2,32,2048]{3,2,1,0:T(8,128)(2,1)} %reference_ref.3), custom_call_target="tpu_custom_call" | custom-call | tf_op jit(solution)/shard_map/pack_body/pallas_call | solution.py:188
  2.7 21.2 %all_to_all.10.message_ref = bf16[16,120,128]{2,1,0:T(8,128)(2,1)} all-to-all(bf16[16,120,128]{2,1,0:T(8,128)(2,1)} %pack_body.1), channel_id=1, replica_groups=mesh['row'=16,'col'=1,'chan'=2] {'row'}, dimensions={0} | all-to-all | bytes 983040 | tf_op jit(solution)/shard_map/all_to_all | solution.py:212
  23.9 2.0 %product_body.1 = f32[8,48,128]{2,1,0:T(8,128)} custom-call(bf16[16,120,128]{2,1,0:T(8,128)(2,1)} %all_to_all.10.message_ref), custom_call_target="tpu_custom_call" | custom-call | tf_op jit(solution)/shard_map/product_body/pallas_call | solution.py:188
  25.9 3.4 %all-to-all-start.1 = ((f32[8,48,128]{2,1,0:T(8,128)}), f32[8,48,128]{2,1,0:T(8,128)S(1)}, u32[]{:S(2)}, u32[]{:S(2)}) async-start(f32[8,48,128]{2,1,0:T(8,128)} %product_body.1), calls=%async_computation.1 | async-start | bytes 393216 | tf_op jit(solution)/shard_map/all_to_all | solution.py:230
  29.3 5.6 %solve_body.1.solved_ref = f32[3,2,32,8]{3,2,1,0:T(8,128)} custom-call(bf16[3,2,8,2048]{3,2,1,0:T(8,128)(2,1)} %volts_ref.3, bf16[3,2,32,2048]{3,2,1,0:T(8,128)(2,1)} %reference_ref.3), custom_call_target="tpu_custom_call" | custom-call | flops 1000000000 | bytes 20000000 | tf_op jit(solution)/shard_map/solve_body/pallas_call | solution.py:188
  34.8 2.4 %correction_body.1.correction_ref = f32[3,2,8,128]{3,2,1,0:T(8,128)} custom-call(bf16[16,120,128]{2,1,0:T(8,128)(2,1)} %all_to_all.10.message_ref, f32[3,2,32,8]{3,2,1,0:T(8,128)} %solve_body.1.solved_ref), custom_call_target="tpu_custom_call" | custom-call | flops 100000000 | bytes 2000000 | tf_op jit(solution)/shard_map/correction_body/pallas_call | solution.py:188
  37.2 0.0 all-to-all-done.1.partial_ref
  37.3 0.0 copy-start
  37.3 0.7 %copy-done = f32[8,48,128]{2,1,0:T(8,128)} copy-done((f32[8,48,128]{2,1,0:T(8,128)}, f32[8,48,128]{2,1,0:T(8,128)S(1)}, u32[]{:S(2)}) %copy-start) | copy-done | bytes 196632
  37.9 1.6 %finish_body.1 = f32[3,2,8,128]{3,2,1,0:T(8,128)} custom-call(f32[8,48,128]{2,1,0:T(8,128)} %copy-done, f32[3,2,8,128]{3,2,1,0:T(8,128)} %correction_body.1.correction_ref), custom_call_target="tpu_custom_call" | custom-call | tf_op jit(solution)/shard_map/finish_body/pallas_call | solution.py:188
Async XLA Ops:
  25.9 11.4 %all-to-all-start.1 = ((f32[8,48,128]{2,1,0:T(8,128)}), f32[8,48,128]{2,1,0:T(8,128)S(1)}, u32[]{:S(2)}, u32[]{:S(2)}) async-start(f32[8,48,128]{2,1,0:T(8,128)} %product_body.1), calls=%async_computation.1 | async-start | bytes 393216 | tf_op jit(solution)/shard_map/all_to_all | solution.py:230
  37.3 0.7 %copy-start = (f32[8,48,128]{2,1,0:T(8,128)}, f32[8,48,128]{2,1,0:T(8,128)S(1)}, u32[]{:S(2)}) copy-start(f32[8,48,128]{2,1,0:T(8,128)S(1)} %all-to-all-done.1.partial_ref) | copy-start | bytes 589828

commit v2 on v1

--- a/solution.py
+++ b/solution.py
@@ -8,6 +8,7 @@
 from jax.sharding import PartitionSpec as P
 
 LANES = 128
+GRANT = 16 * 1024 * 1024
 NT = (((1,), (1,)), ((), ()))
 TN = (((0,), (0,)), ((), ()))
 TT = (((0,), (1,)), ((), ()))
@@ -72,12 +73,25 @@
     return jnp.stack(results)
 
 
-def pack_body(volts_ref, reference_ref, message_ref, *, group):
+def pack_body(volts_ref, message_ref, *, group):
     subs, _, ants, samples = volts_ref.shape
     members = message_ref.shape[0]
     share = samples // group
     tiles = share // LANES
-    base = subs * 2 * tiles * ants
+    for s in range(subs):
+        for p in range(2):
+            for c in range(group):
+                for t in range(tiles):
+                    at = ((s * 2 + p) * tiles + t) * ants
+                    start = c * share + t * LANES
+                    block = volts_ref[s, p, :, start : start + LANES]
+                    for m in range(c, members, group):
+                        message_ref[m, at : at + ants, :] = block
+
+
+def cross_body(volts_ref, reference_ref, message_ref):
+    subs, _, ants, samples = volts_ref.shape
+    crosses = []
     for s in range(subs):
         real, imag = volts_ref[s, 0], volts_ref[s, 1]
         ref_real, ref_imag = reference_ref[s, 0], reference_ref[s, 1]
@@ -86,17 +100,13 @@
         ) + lax.dot_general(
             imag, jnp.concatenate([ref_imag, ref_real], 0), NT, preferred_element_type=jnp.float32
         )
-        cross = cross / jnp.float32(samples)
-        high = cross.astype(jnp.bfloat16)
-        low = (cross - high.astype(jnp.float32)).astype(jnp.bfloat16)
-        both = jnp.concatenate([high, low], 1)
-        for m in range(members):
-            message_ref[m, base + s * ants : base + (s + 1) * ants, :] = both
-            for p in range(2):
-                for t in range(tiles):
-                    at = ((s * 2 + p) * tiles + t) * ants
-                    start = (m % group) * share + t * LANES
-                    message_ref[m, at : at + ants, :] = volts_ref[s, p, :, start : start + LANES]
+        crosses.append(cross / jnp.float32(samples))
+    if subs % 2:
+        crosses.append(jnp.zeros_like(crosses[0]))
+    for pair in range(len(crosses) // 2):
+        message_ref[0, pair * ants : (pair + 1) * ants, :] = jnp.concatenate(
+            crosses[2 * pair : 2 * pair + 2], 1
+        )
 
 
 def solve_body(volts_ref, reference_ref, solved_ref):
@@ -136,7 +146,7 @@
 def product_body(message_ref, partial_ref, *, group, subs, ants):
     members = message_ref.shape[0]
     rows = partial_ref.shape[1] // (subs * 2)
-    tiles = (message_ref.shape[1] // ants - subs) // (subs * 2)
+    tiles = message_ref.shape[1] // (ants * subs * 2)
     mine = (lax.axis_index("row") // group) * group
     for s in range(subs):
         cols, own = [], []
@@ -158,17 +168,37 @@
             )
 
 
-def correction_body(message_ref, solved_ref, correction_ref):
+def correction_body(cross_ref, solved_ref, correction_ref):
     subs, _, nref, ants = solved_ref.shape
-    base = message_ref.shape[1] - subs * ants
-    for s in range(subs):
-        cross = joined(message_ref[:, base + s * ants : base + (s + 1) * ants, :])
-        re, im = solved_ref[s, 0], solved_ref[s, 1]
-        for p, stack in enumerate(([re, -im], [-im, -re])):
-            column = jnp.concatenate(stack + stack, 0)
-            correction_ref[s, p] = lax.dot_general(
-                column, cross, TT, precision=HIGHEST, preferred_element_type=jnp.float32
-            )
+    me = lax.axis_index("row")
+    for pair in range((subs + 1) // 2):
+        members = range(2 * pair, min(2 * pair + 2, subs))
+        cross = jnp.concatenate(
+            [
+                cross_ref[jnp.bitwise_xor(me, j), pair * ants : (pair + 1) * ants, :]
+                for j in range(cross_ref.shape[0])
+            ],
+            0,
+        )
+        columns = []
+        for s in members:
+            re, im = solved_ref[s, 0], solved_ref[s, 1]
+            none = jnp.zeros((2 * nref, ants), jnp.float32)
+            for stack in ([re, -im], [-im, -re]):
+                columns.append(
+                    jnp.concatenate(stack + [none] if s % 2 == 0 else [none] + stack, 0)
+                )
+        out = lax.dot_general(
+            jnp.concatenate(columns, 1),
+            cross,
+            TT,
+            precision=HIGHEST,
+            preferred_element_type=jnp.float32,
+        )
+        for k, s in enumerate(members):
+            for p in range(2):
+                at = (2 * k + p) * ants
+                correction_ref[s, p] = out[at : at + ants]
 
 
 def finish_body(partial_ref, correction_ref, cleaned_ref, *, samples):
@@ -183,13 +213,18 @@
             cleaned_ref[s, p] = total[at : at + ants] - correction_ref[s, p]
 
 
-def call(body, out, *args, flops=0, moved=0, **kw):
+def call(body, out, *args, inner=(), flops=0, moved=0, **kw):
     spec = pl.BlockSpec(memory_space=pltpu.VMEM)
+    args = [
+        pltpu.with_memory_space_constraint(x, pltpu.VMEM) if i in inner else x
+        for i, x in enumerate(args)
+    ]
     return pl.pallas_call(
         functools.partial(body, **kw) if kw else body,
         out_shape=out,
         in_specs=[spec] * len(args),
         out_specs=spec,
+        compiler_params=pltpu.CompilerParams(vmem_limit_bytes=GRANT),
         cost_estimate=pl.CostEstimate(flops=flops, bytes_accessed=moved, transcendentals=0),
         name=body.__name__,
     )(*args)
@@ -200,19 +235,33 @@
     nref = reference_volts.shape[2]
     group = n_row // 2
     tiles = samples // group // LANES
-    f32 = functools.partial(jax.ShapeDtypeStruct, dtype=jnp.float32)
-    height = subs * 2 * tiles * ants + subs * ants
+    f32 = jnp.float32
+    height = subs * 2 * tiles * ants
     message = call(
         pack_body,
         jax.ShapeDtypeStruct((n_row, height, LANES), jnp.bfloat16),
         array_volts,
+        group=group,
+    )
+    volts = lax.all_to_all(message, "row", split_axis=0, concat_axis=0, tiled=True)
+    crosses = call(
+        cross_body,
+        jax.ShapeDtypeStruct((1, (subs + 1) // 2 * ants, LANES), f32),
+        array_volts,
         reference_volts,
-        group=group,
-    )
-    volts = lax.all_to_all(message, "row", split_axis=0, concat_axis=0, tiled=True)
+        flops=10**8,
+        moved=10**6,
+    )
+    bit = 1
+    while bit < n_row:
+        other = lax.ppermute(crosses, "row", [(i, i ^ bit) for i in range(n_row)])
+        if 2 * bit == n_row:
+            volts, crosses = lax.optimization_barrier((volts, crosses))
+        crosses = jnp.concatenate([crosses, other], 0)
+        bit *= 2
     solved = call(
         solve_body,
-        f32((subs, 2, nref, ants)),
+        pltpu.VMEM((subs, 2, nref, ants), f32),
         array_volts,
         reference_volts,
         flops=10**9,
@@ -220,8 +269,9 @@
     )
     partial = call(
         product_body,
-        f32((group, subs * 2 * ants, n_row * ants)),
+        pltpu.VMEM((group, subs * 2 * ants, n_row * ants), f32),
         volts,
+        inner=(0,),
         group=group,
         subs=subs,
         ants=ants,
@@ -232,14 +282,20 @@
     )
     correction = call(
         correction_body,
-        f32((subs, 2, ants, n_row * ants)),
-        volts,
+        pltpu.VMEM((subs, 2, ants, n_row * ants), f32),
+        crosses,
         solved,
+        inner=(0, 1),
         flops=10**8,
         moved=2 * 10**6,
     )
     return call(
-        finish_body, f32((subs, 2, ants, n_row * ants)), sums, correction, samples=samples
+        finish_body,
+        jax.ShapeDtypeStruct((subs, 2, ants, n_row * ants), f32),
+        sums,
+        correction,
+        inner=(0, 1),
+        samples=samples,
     )
 
 
@@ -249,7 +305,7 @@
     def body(array_volts, reference_volts):
         samples = array_volts.shape[3]
         nref = reference_volts.shape[2]
-        split = n_col == 1 and n_row % 2 == 0 and samples % (n_row // 2 * LANES) == 0
+        split = n_col == 1 and n_row > 1 and n_row & (n_row - 1) == 0 and samples % (n_row // 2 * LANES) == 0
         if split and 4 * nref == LANES:
             return per_device(array_volts, reference_volts, n_row=n_row)
         return per_device_any(array_volts, reference_volts)

time: 39.9 us -> 34.2 us (0.86)
  blocking collectives: 21.2 us -> 0 us
  starting transfers between devices: 3.39 us -> 16.1 us
  waiting for transfers between devices: 0.01 us -> 9.66 us
  Pallas kernels: 14.2 us -> 7.05 us
    all_to_all x1 -> x0, blocking collectives: 21.2 us -> none  [per_device(): lax.all_to_all(message, 'row', split_axis=0, concat_axis=0, tiled=True)]
    all_to_all x0 -> x1, starting transfers between devices: none -> 7.52 us  [per_device(): lax.all_to_all(message, 'row', split_axis=0, concat_axis=0, tiled=True)]
    pallas_call x5 -> x6, Pallas kernels: 14.2 us -> 7.05 us  [call(): pl.pallas_call(functools.partial(body, **kw) if kw else body, out_shape=o...]
    ppermute x0 -> x4, waiting for transfers between devices: none -> 5.88 us  [per_device(): other = lax.ppermute(crosses, 'row', [(i, i ^ bit) for i in range(n_row)])]
    ppermute x0 -> x4, starting transfers between devices: none -> 5.22 us  [per_device(): other = lax.ppermute(crosses, 'row', [(i, i ^ bit) for i in range(n_row)])]
    all_to_all x0 -> x1, waiting for transfers between devices: none -> 2.59 us  [per_device(): lax.all_to_all(message, 'row', split_axis=0, concat_axis=0, tiled=True)]
    all_to_all x1, waiting for transfers between devices: 0.01 us -> 1.19 us  [per_device(): lax.all_to_all(partial, 'row', split_axis=0, concat_axis=0, tiled=True, a...]
    unnamed x2 -> x6, local copies, waits for them, and re-layouts: 0.67 us -> 0.93 us
  transfers between devices with their start and end apart: 1 -> 6, of which waited for: 0 -> 6; matrix products, arithmetic and copies ran while one was open for 0% -> 0% of each run, Pallas kernels for 20% -> 14%
where the time goes in v2:
time: 34.2 us; the launch traced here: 33.9 us
  starting transfers between devices  16.1 us (47%)
  waiting for transfers between devices  9.66 us (28%)
  Pallas kernels  7.05 us (21%)
  local copies, waits for them, and re-layouts  0.93 us (3%)
    all_to_all x1, starting transfers between devices, per_device(): lax.all_to_all(message, 'row', split_axis=0, concat_axis=0, tiled=True)  7.52 us
    pallas_call x6, Pallas kernels, call(): pl.pallas_call(functools.partial(body, **kw) if kw else body, out_shape=o...  7.05 us
    ppermute x4, waiting for transfers between devices, per_device(): other = lax.ppermute(crosses, 'row', [(i, i ^ bit) for i in range(n_row)])  5.88 us
    ppermute x4, starting transfers between devices, per_device(): other = lax.ppermute(crosses, 'row', [(i, i ^ bit) for i in range(n_row)])  5.22 us
    all_to_all x1, starting transfers between devices, per_device(): lax.all_to_all(partial, 'row', split_axis=0, concat_axis=0, tiled=True, a...  3.39 us
    all_to_all x1, waiting for transfers between devices, per_device(): lax.all_to_all(message, 'row', split_axis=0, concat_axis=0, tiled=True)  2.59 us
    all_to_all x1, waiting for transfers between devices, per_device(): lax.all_to_all(partial, 'row', split_axis=0, concat_axis=0, tiled=True, a...  1.19 us
    unnamed x6, local copies, waits for them, and re-layouts  0.93 us
  transfers between devices with their start and end apart: 6, of which 6 were waited for; matrix products, arithmetic and copies ran while one was open for 0% of the time, Pallas kernels for 14%

profile of v2, /device:TPU:0, one launch (start us, length us, event | category | flops | bytes accessed | tf_op | source)
XLA Modules:
  0.0 33.9 jit_solution(15947757634606373389)
XLA Ops:
  0.0 0.0 copy-start.1
  0.0 0.9 %copy-done.1 = bf16[3,2,8,2048]{3,2,1,0:T(8,128)(2,1)S(1)} copy-done((bf16[3,2,8,2048]{3,2,1,0:T(8,128)(2,1)S(1)}, bf16[3,2,8,2048]{3,2,1,0:T(8,128)(2,1)}, u32[]{:S(2)}) %copy-start.1) | copy-done | bytes 196632
  0.9 0.0 copy-start
  0.9 0.8 %pack_body.1 = bf16[16,96,128]{2,1,0:T(8,128)(2,1)} custom-call(bf16[3,2,8,2048]{3,2,1,0:T(8,128)(2,1)S(1)} %copy-done.1), custom_call_target="tpu_custom_call" | custom-call | tf_op jit(solution)/shard_map/pack_body/pallas_call | solution.py:222
  1.7 0.0 copy-start.2
  1.7 7.5 %all-to-all-start = ((bf16[16,96,128]{2,1,0:T(8,128)(2,1)}), bf16[16,96,128]{2,1,0:T(8,128)(2,1)S(1)}, u32[]{:S(2)}, u32[]{:S(2)}) async-start(bf16[16,96,128]{2,1,0:T(8,128)(2,1)} %pack_body.1), calls=%async_computation | async-start | bytes 786432 | tf_op jit(solution)/shard_map/all_to_all | solution.py:246
  9.3 0.0 copy-done
  9.3 0.0 copy-done.2
  9.3 0.6 %cross_body.1 = f32[1,16,128]{2,1,0:T(8,128)S(1)} custom-call(bf16[3,2,8,2048]{3,2,1,0:T(8,128)(2,1)S(1)} %copy-done.2, bf16[3,2,32,2048]{3,2,1,0:T(8,128)(2,1)S(1)} %copy-done), custom_call_target="tpu_custom_call" | custom-call | flops 100000000 | bytes 1000000 | tf_op jit(solution)/shard_map/cross_body/pallas_call | solution.py:222
  9.9 0.4 %collective-permute-start = (f32[1,16,128]{2,1,0:T(8,128)S(1)}, f32[1,16,128]{2,1,0:T(8,128)S(1)}, u32[]{:S(2)}, u32[]{:S(2)}) collective-permute-start(f32[1,16,128]{2,1,0:T(8,128)S(1)} %cross_body.1), channel_id=1, source_target_pairs={{0,2},{2,0},{4,6},{6,4},{8,10},{10,8},{12,14},{14,12},{16,18},{18,... | collective-permute-start | bytes 24584 | tf_op jit(solution)/shard_map/ppermute | solution.py:257
  10.3 0.8 %collective-permute-done = f32[1,16,128]{2,1,0:T(8,128)S(1)} collective-permute-done((f32[1,16,128]{2,1,0:T(8,128)S(1)}, f32[1,16,128]{2,1,0:T(8,128)S(1)}, u32[]{:S(2)}, u32[]{:S(2)}) %collective-permute-start) | collective-permute-done | bytes 8224 | tf_op jit(solution)/shard_map/ppermute | solution.py:257
  11.1 1.9 %collective-permute-start.1 = (f32[2,16,128]{2,1,0:T(8,128)S(1)}, f32[2,16,128]{2,1,0:T(8,128)S(1)}, u32[]{:S(2)}, u32[]{:S(2)}) collective-permute-start(f32[2,16,128]{2,1,0:T(8,128)S(1)} %pad_maximum_fusion.3), channel_id=1, source_target_pairs={{0,4},{2,6},{4,0},{6,2},{8,12},{10,14},{12,8},{14,10},{16,20},{18,... | collective-permute-start | bytes 49160 | tf_op jit(solution)/shard_map/ppermute | solution.py:257
  13.0 2.1 %collective-permute-done.1 = f32[2,16,128]{2,1,0:T(8,128)S(1)} collective-permute-done((f32[2,16,128]{2,1,0:T(8,128)S(1)}, f32[2,16,128]{2,1,0:T(8,128)S(1)}, u32[]{:S(2)}, u32[]{:S(2)}) %collective-permute-start.1) | collective-permute-done | bytes 16416 | tf_op jit(solution)/shard_map/ppermute | solution.py:257
  15.1 1.6 %collective-permute-start.2 = (f32[4,16,128]{2,1,0:T(8,128)S(1)}, f32[4,16,128]{2,1,0:T(8,128)S(1)}, u32[]{:S(2)}, u32[]{:S(2)}) collective-permute-start(f32[4,16,128]{2,1,0:T(8,128)S(1)} %pad_maximum_fusion.2), channel_id=1, source_target_pairs={{0,8},{2,10},{4,12},{6,14},{8,0},{10,2},{12,4},{14,6},{16,24},{18,... | collective-permute-start | bytes 98312 | tf_op jit(solution)/shard_map/ppermute | solution.py:257
  16.7 2.6 %collective-permute-done.2 = f32[4,16,128]{2,1,0:T(8,128)S(1)} collective-permute-done((f32[4,16,128]{2,1,0:T(8,128)S(1)}, f32[4,16,128]{2,1,0:T(8,128)S(1)}, u32[]{:S(2)}, u32[]{:S(2)}) %collective-permute-start.2) | collective-permute-done | bytes 32800 | tf_op jit(solution)/shard_map/ppermute | solution.py:257
  19.3 2.6 %all-to-all-done.message_ref = bf16[16,96,128]{2,1,0:T(8,128)(2,1)S(1)} async-done(((bf16[16,96,128]{2,1,0:T(8,128)(2,1)}), bf16[16,96,128]{2,1,0:T(8,128)(2,1)S(1)}, u32[]{:S(2)}, u32[]{:S(2)}) %all-to-all-start) | async-done | bytes 393248 | tf_op jit(solution)/shard_map/all_to_all | solution.py:246
  21.9 0.9 %product_body.1 = f32[8,48,128]{2,1,0:T(8,128)} custom-call(bf16[16,96,128]{2,1,0:T(8,128)(2,1)S(1)} %all-to-all-done.message_ref), custom_call_target="tpu_custom_call" | custom-call | tf_op jit(solution)/shard_map/product_body/pallas_call | solution.py:222
  22.8 3.4 %all-to-all-start.1 = ((f32[8,48,128]{2,1,0:T(8,128)}), f32[8,48,128]{2,1,0:T(8,128)S(1)}, u32[]{:S(2)}, u32[]{:S(2)}) async-start(f32[8,48,128]{2,1,0:T(8,128)} %product_body.1), calls=%async_computation.1 | async-start | bytes 393216 | tf_op jit(solution)/shard_map/all_to_all | solution.py:280
  26.2 1.3 %collective-permute-start.3 = (f32[8,16,128]{2,1,0:T(8,128)S(1)}, f32[8,16,128]{2,1,0:T(8,128)S(1)}, u32[]{:S(2)}, u32[]{:S(2)}) collective-permute-start(f32[8,16,128]{2,1,0:T(8,128)S(1)} %pad_maximum_fusion.1), channel_id=1, source_target_pairs={{0,16},{2,18},{4,20},{6,22},{8,24},{10,26},{12,28},{14,30},{16,0},... | collective-permute-start | bytes 196616 | tf_op jit(solution)/shard_map/ppermute | solution.py:257
  27.5 3.7 %solve_body.1.solved_ref = f32[3,2,32,8]{3,2,1,0:T(8,128)S(1)} custom-call(bf16[3,2,8,2048]{3,2,1,0:T(8,128)(2,1)S(1)} %copy-done.2, bf16[3,2,32,2048]{3,2,1,0:T(8,128)(2,1)S(1)} %copy-done), custom_call_target="tpu_custom_call" | custom-call | flops 1000000000 | bytes 20000000 | tf_op jit(solution)/shard_map/solve_body/pallas_call | solution.py:222
  31.2 0.4 %collective-permute-done.3 = f32[8,16,128]{2,1,0:T(8,128)S(1)} collective-permute-done((f32[8,16,128]{2,1,0:T(8,128)S(1)}, f32[8,16,128]{2,1,0:T(8,128)S(1)}, u32[]{:S(2)}, u32[]{:S(2)}) %collective-permute-start.3) | collective-permute-done | bytes 65568 | tf_op jit(solution)/shard_map/ppermute | solution.py:257
  31.6 0.4 %correction_body.1.correction_ref = f32[3,2,8,128]{3,2,1,0:T(8,128)S(1)} custom-call(f32[16,16,128]{2,1,0:T(8,128)S(1)} %pad_maximum_fusion.cross_ref, f32[3,2,32,8]{3,2,1,0:T(8,128)S(1)} %solve_body.1.solved_ref), custom_call_target="tpu_custom_call" | custom-call | flops 100000000 | bytes 2000000 | tf_op jit(solution)/shard_map/correction_body/pallas_call | solution.py:222
  32.0 1.2 %all-to-all-done.1.partial_ref = f32[8,48,128]{2,1,0:T(8,128)S(1)} async-done(((f32[8,48,128]{2,1,0:T(8,128)}), f32[8,48,128]{2,1,0:T(8,128)S(1)}, u32[]{:S(2)}, u32[]{:S(2)}) %all-to-all-start.1) | async-done | bytes 196640 | tf_op jit(solution)/shard_map/all_to_all | solution.py:280
  33.2 0.6 %finish_body.1 = f32[3,2,8,128]{3,2,1,0:T(8,128)} custom-call(f32[8,48,128]{2,1,0:T(8,128)S(1)} %all-to-all-done.1.partial_ref, f32[3,2,8,128]{3,2,1,0:T(8,128)S(1)} %correction_body.1.correction_ref), custom_call_target="tpu_custom_call" | custom-call | tf_op jit(solution)/shard_map/finish_body/pallas_call | solution.py:222
  (4 shorter events, 0.0 us)
Async XLA Ops:
  0.0 0.9 %copy-start.1 = (bf16[3,2,8,2048]{3,2,1,0:T(8,128)(2,1)S(1)}, bf16[3,2,8,2048]{3,2,1,0:T(8,128)(2,1)}, u32[]{:S(2)}) copy-start(bf16[3,2,8,2048]{3,2,1,0:T(8,128)(2,1)} %volts_ref.5) | copy-start | bytes 589828
  0.9 8.3 %copy-start = (bf16[3,2,32,2048]{3,2,1,0:T(8,128)(2,1)S(1)}, bf16[3,2,32,2048]{3,2,1,0:T(8,128)(2,1)}, u32[]{:S(2)}) copy-start(bf16[3,2,32,2048]{3,2,1,0:T(8,128)(2,1)} %reference_ref.3) | copy-start | bytes 2359300
  1.7 7.5 %copy-start.2 = (bf16[3,2,8,2048]{3,2,1,0:T(8,128)(2,1)S(1)}, bf16[3,2,8,2048]{3,2,1,0:T(8,128)(2,1)}, u32[]{:S(2)}) copy-start(bf16[3,2,8,2048]{3,2,1,0:T(8,128)(2,1)} %volts_ref.5) | copy-start | bytes 589828
  1.7 20.1 %all-to-all-start = ((bf16[16,96,128]{2,1,0:T(8,128)(2,1)}), bf16[16,96,128]{2,1,0:T(8,128)(2,1)S(1)}, u32[]{:S(2)}, u32[]{:S(2)}) async-start(bf16[16,96,128]{2,1,0:T(8,128)(2,1)} %pack_body.1), calls=%async_computation | async-start | bytes 786432 | tf_op jit(solution)/shard_map/all_to_all | solution.py:246
  9.9 1.2 %collective-permute-start = (f32[1,16,128]{2,1,0:T(8,128)S(1)}, f32[1,16,128]{2,1,0:T(8,128)S(1)}, u32[]{:S(2)}, u32[]{:S(2)}) collective-permute-start(f32[1,16,128]{2,1,0:T(8,128)S(1)} %cross_body.1), channel_id=1, source_target_pairs={{0,2},{2,0},{4,6},{6,4},{8,10},{10,8},{12,14},{14,12},{16,18},{18,... | collective-permute-start | bytes 24584 | tf_op jit(solution)/shard_map/ppermute | solution.py:257
  11.1 4.0 %collective-permute-start.1 = (f32[2,16,128]{2,1,0:T(8,128)S(1)}, f32[2,16,128]{2,1,0:T(8,128)S(1)}, u32[]{:S(2)}, u32[]{:S(2)}) collective-permute-start(f32[2,16,128]{2,1,0:T(8,128)S(1)} %pad_maximum_fusion.3), channel_id=1, source_target_pairs={{0,4},{2,6},{4,0},{6,2},{8,12},{10,14},{12,8},{14,10},{16,20},{18,... | collective-permute-start | bytes 49160 | tf_op jit(solution)/shard_map/ppermute | solution.py:257
  15.1 4.2 %collective-permute-start.2 = (f32[4,16,128]{2,1,0:T(8,128)S(1)}, f32[4,16,128]{2,1,0:T(8,128)S(1)}, u32[]{:S(2)}, u32[]{:S(2)}) collective-permute-start(f32[4,16,128]{2,1,0:T(8,128)S(1)} %pad_maximum_fusion.2), channel_id=1, source_target_pairs={{0,8},{2,10},{4,12},{6,14},{8,0},{10,2},{12,4},{14,6},{16,24},{18,... | collective-permute-start | bytes 98312 | tf_op jit(solution)/shard_map/ppermute | solution.py:257
  22.8 10.4 %all-to-all-start.1 = ((f32[8,48,128]{2,1,0:T(8,128)}), f32[8,48,128]{2,1,0:T(8,128)S(1)}, u32[]{:S(2)}, u32[]{:S(2)}) async-start(f32[8,48,128]{2,1,0:T(8,128)} %product_body.1), calls=%async_computation.1 | async-start | bytes 393216 | tf_op jit(solution)/shard_map/all_to_all | solution.py:280
  26.2 5.4 %collective-permute-start.3 = (f32[8,16,128]{2,1,0:T(8,128)S(1)}, f32[8,16,128]{2,1,0:T(8,128)S(1)}, u32[]{:S(2)}, u32[]{:S(2)}) collective-permute-start(f32[8,16,128]{2,1,0:T(8,128)S(1)} %pad_maximum_fusion.1), channel_id=1, source_target_pairs={{0,16},{2,18},{4,20},{6,22},{8,24},{10,26},{12,28},{14,30},{16,0},... | collective-permute-start | bytes 196616 | tf_op jit(solution)/shard_map/ppermute | solution.py:257

commit v3 on v2

--- a/solution.py
+++ b/solution.py
@@ -109,23 +109,34 @@
         )
 
 
-def solve_body(volts_ref, reference_ref, solved_ref):
+def system_body(volts_ref, reference_ref, system_ref):
     subs, _, ants, samples = volts_ref.shape
     nref = reference_ref.shape[2]
+    dot = functools.partial(
+        lax.dot_general, dimension_numbers=NT, preferred_element_type=jnp.float32
+    )
     reals, imags = [], []
     for s in range(subs):
         real, imag = volts_ref[s, 0], volts_ref[s, 1]
         ref_real, ref_imag = reference_ref[s, 0], reference_ref[s, 1]
         first = jnp.concatenate([ref_real, real], 0)
         second = jnp.concatenate([ref_imag, imag], 0)
-        dot = functools.partial(
-            lax.dot_general, dimension_numbers=NT, preferred_element_type=jnp.float32
-        )
         reals.append((dot(ref_real, first) + dot(ref_imag, second)) / jnp.float32(samples))
         imags.append((dot(ref_imag, first) - dot(ref_real, second)) / jnp.float32(samples))
-    re, im = jnp.stack(reals), jnp.stack(imags)
-    rows = lax.broadcasted_iota(jnp.int32, (1, nref, 1), 1)
-    for i in range(nref):
+    re, im = eliminate(jnp.stack(reals), jnp.stack(imags), 0, nref // 2)
+    system_ref[0], system_ref[1] = re, im
+
+
+def solve_body(system_ref, solved_ref):
+    nref = system_ref.shape[2]
+    re, im = eliminate(system_ref[0], system_ref[1], nref // 2, nref)
+    solved_ref[:, 0] = re[:, :, nref:]
+    solved_ref[:, 1] = im[:, :, nref:]
+
+
+def eliminate(re, im, start, stop):
+    rows = lax.broadcasted_iota(jnp.int32, (1, re.shape[1], 1), 1)
+    for i in range(start, stop):
         inverse = 1.0 / re[:, i : i + 1, i : i + 1]
         row_re, row_im = re[:, i : i + 1, :] * inverse, im[:, i : i + 1, :] * inverse
         col_re, col_im = re[:, :, i : i + 1], im[:, :, i : i + 1]
@@ -134,8 +145,7 @@
             jnp.where(here, row_re, re - (col_re * row_re - col_im * row_im)),
             jnp.where(here, row_im, im - (col_re * row_im + col_im * row_re)),
         )
-    solved_ref[:, 0] = re[:, :, nref:]
-    solved_ref[:, 1] = im[:, :, nref:]
+    return re, im
 
 
 def joined(block):
@@ -143,29 +153,36 @@
     return block.astype(jnp.float32).reshape(members * ants, lanes)
 
 
-def product_body(message_ref, partial_ref, *, group, subs, ants):
+def product_body(message_ref, even_ref, odd_ref, *, group, subs, ants):
     members = message_ref.shape[0]
-    rows = partial_ref.shape[1] // (subs * 2)
     tiles = message_ref.shape[1] // (ants * subs * 2)
-    mine = (lax.axis_index("row") // group) * group
+    me = lax.axis_index("row")
     for s in range(subs):
         cols, own = [], []
         for p in range(2):
             for t in range(tiles):
                 at = ((s * 2 + p) * tiles + t) * ants
                 cols.append(joined(message_ref[:, at : at + ants, :]).astype(jnp.bfloat16))
-                own.append(joined(message_ref[pl.ds(mine, group), at : at + ants, :]))
+                own.append(
+                    jnp.concatenate(
+                        [
+                            message_ref[me ^ j, at : at + ants, :].astype(jnp.float32)
+                            for j in range(group)
+                        ],
+                        0,
+                    )
+                )
         right = jnp.concatenate(cols, 1)
         upper = jnp.concatenate(own, 1)
         lower = jnp.concatenate(own[tiles:] + [-x for x in own[:tiles]], 1)
         left = jnp.concatenate([upper, lower], 0).astype(jnp.bfloat16)
         out = lax.dot_general(left, right, NT, preferred_element_type=jnp.float32)
-        height = group * ants
         for p in range(2):
-            at = (s * 2 + p) * rows
-            partial_ref[:, at : at + rows, :] = out[p * height : (p + 1) * height].reshape(
-                group, ants, members * ants
-            )
+            at = (s * 2 + p) * ants
+            for j in range(group):
+                row = (p * group + j) * ants
+                ref = odd_ref if j % 2 else even_ref
+                ref[j // 2, at : at + ants, :] = out[row : row + ants]
 
 
 def correction_body(cross_ref, solved_ref, correction_ref):
@@ -175,8 +192,8 @@
         members = range(2 * pair, min(2 * pair + 2, subs))
         cross = jnp.concatenate(
             [
-                cross_ref[jnp.bitwise_xor(me, j), pair * ants : (pair + 1) * ants, :]
-                for j in range(cross_ref.shape[0])
+                cross_ref[me ^ m, pair * ants : (pair + 1) * ants, :]
+                for m in range(cross_ref.shape[0])
             ],
             0,
         )
@@ -201,16 +218,21 @@
                 correction_ref[s, p] = out[at : at + ants]
 
 
-def finish_body(partial_ref, correction_ref, cleaned_ref, *, samples):
+def finish_body(kept_ref, *refs, samples):
+    *others, correction_ref, cleaned_ref = refs
     subs, _, ants, _ = cleaned_ref.shape
-    total = partial_ref[0]
-    for m in range(1, partial_ref.shape[0]):
-        total = total + partial_ref[m]
+    total = kept_ref[0]
+    for ref in others:
+        total = total + ref[0]
     total = total / jnp.float32(samples)
     for s in range(subs):
         for p in range(2):
             at = (s * 2 + p) * ants
             cleaned_ref[s, p] = total[at : at + ants] - correction_ref[s, p]
+
+
+def swap(x, bit, n_row):
+    return lax.ppermute(x, "row", [(i, i ^ bit) for i in range(n_row)])
 
 
 def call(body, out, *args, inner=(), flops=0, moved=0, **kw):
@@ -223,7 +245,7 @@
         functools.partial(body, **kw) if kw else body,
         out_shape=out,
         in_specs=[spec] * len(args),
-        out_specs=spec,
+        out_specs=[spec] * len(out) if isinstance(out, list) else spec,
         compiler_params=pltpu.CompilerParams(vmem_limit_bytes=GRANT),
         cost_estimate=pl.CostEstimate(flops=flops, bytes_accessed=moved, transcendentals=0),
         name=body.__name__,
@@ -254,32 +276,42 @@
     )
     bit = 1
     while bit < n_row:
-        other = lax.ppermute(crosses, "row", [(i, i ^ bit) for i in range(n_row)])
-        if 2 * bit == n_row:
+        last = 2 * bit == n_row
+        if last:
             volts, crosses = lax.optimization_barrier((volts, crosses))
+        with jax.named_scope("last_hop" if last else "hop"):
+            other = swap(crosses, bit, n_row)
         crosses = jnp.concatenate([crosses, other], 0)
         bit *= 2
-    solved = call(
-        solve_body,
-        pltpu.VMEM((subs, 2, nref, ants), f32),
+    system = call(
+        system_body,
+        pltpu.VMEM((2, subs, nref, nref + ants), f32),
         array_volts,
         reference_volts,
         flops=10**9,
         moved=2 * 10**7,
     )
-    partial = call(
+    solved = call(
+        solve_body,
+        pltpu.VMEM((subs, 2, nref, ants), f32),
+        system,
+        inner=(0,),
+        flops=10**9,
+        moved=2 * 10**7,
+    )
+    volts, solved = lax.optimization_barrier((volts, solved))
+    half = pltpu.VMEM((group // 2, subs * 2 * ants, n_row * ants), f32)
+    even, odd = call(
         product_body,
-        pltpu.VMEM((group, subs * 2 * ants, n_row * ants), f32),
+        [half, half],
         volts,
         inner=(0,),
         group=group,
         subs=subs,
         ants=ants,
     )
-    groups = [list(range(group)), list(range(group, n_row))]
-    sums = lax.all_to_all(
-        partial, "row", split_axis=0, concat_axis=0, tiled=True, axis_index_groups=groups
-    )
+    sums = even + swap(odd, 1, n_row)
+    parts = [sums[:1]] + [swap(sums[k : k + 1], 2 * k, n_row) for k in range(1, group // 2)]
     correction = call(
         correction_body,
         pltpu.VMEM((subs, 2, ants, n_row * ants), f32),
@@ -292,9 +324,9 @@
     return call(
         finish_body,
         jax.ShapeDtypeStruct((subs, 2, ants, n_row * ants), f32),
-        sums,
+        *parts,
         correction,
-        inner=(0, 1),
+        inner=range(len(parts) + 1),
         samples=samples,
     )
 

time: 34.2 us -> 31.1 us (0.909)
  waiting for transfers between devices: 9.66 us -> 7.12 us
  Pallas kernels: 7.05 us -> 6.37 us
    ppermute x4 -> x8, starting transfers between devices: 5.22 us -> 8.82 us  [swap(): return lax.ppermute(x, 'row', [(i, i ^ bit) for i in range(n_row)])]
    all_to_all x1 -> x0, starting transfers between devices: 3.39 us -> none  [per_device(): lax.all_to_all(partial, 'row', split_axis=0, concat_axis=0, tiled=True, a...]
    ppermute x4 -> x8, waiting for transfers between devices: 5.88 us -> 4.59 us  [swap(): return lax.ppermute(x, 'row', [(i, i ^ bit) for i in range(n_row)])]
    all_to_all x1 -> x0, waiting for transfers between devices: 1.19 us -> none  [per_device(): lax.all_to_all(partial, 'row', split_axis=0, concat_axis=0, tiled=True, a...]
    pallas_call x6 -> x7, Pallas kernels: 7.05 us -> 6.37 us  [call(): pl.pallas_call(functools.partial(body, **kw) if kw else body, out_shape=o...]
  transfers between devices with their start and end apart: 6 -> 9, of which waited for: 6 -> 5; matrix products, arithmetic and copies ran while one was open for 0% -> 0% of each run, Pallas kernels for 14% -> 15%
where the time goes in v3:
time: 31.1 us; the launch traced here: 30.9 us
  starting transfers between devices  16.3 us (52%)
  waiting for transfers between devices  7.12 us (23%)
  Pallas kernels  6.37 us (20%)
  local copies, waits for them, and re-layouts  0.94 us (3%)
    ppermute x8, starting transfers between devices, swap(): return lax.ppermute(x, 'row', [(i, i ^ bit) for i in range(n_row)])  8.82 us
    all_to_all x1, starting transfers between devices, per_device(): lax.all_to_all(message, 'row', split_axis=0, concat_axis=0, tiled=True)  7.52 us
    pallas_call x7, Pallas kernels, call(): pl.pallas_call(functools.partial(body, **kw) if kw else body, out_shape=o...  6.37 us
    ppermute x8, waiting for transfers between devices, swap(): return lax.ppermute(x, 'row', [(i, i ^ bit) for i in range(n_row)])  4.59 us
    all_to_all x1, waiting for transfers between devices, per_device(): lax.all_to_all(message, 'row', split_axis=0, concat_axis=0, tiled=True)  2.53 us
    unnamed x6, local copies, waits for them, and re-layouts  0.93 us
  transfers between devices with their start and end apart: 9, of which 5 were waited for; matrix products, arithmetic and copies ran while one was open for 0% of the time, Pallas kernels for 15%

profile of v3, /device:TPU:0, one launch (start us, length us, event | category | flops | bytes accessed | tf_op | source)
XLA Modules:
  0.0 30.9 jit_solution(13307685189654556191)
XLA Ops:
  0.0 0.9 %copy-done.1 = bf16[3,2,8,2048]{3,2,1,0:T(8,128)(2,1)S(1)} copy-done((bf16[3,2,8,2048]{3,2,1,0:T(8,128)(2,1)S(1)}, bf16[3,2,8,2048]{3,2,1,0:T(8,128)(2,1)}, u32[]{:S(2)}) %copy-start.1) | copy-done | bytes 196632
  0.9 0.8 %pack_body.1 = bf16[16,96,128]{2,1,0:T(8,128)(2,1)} custom-call(bf16[3,2,8,2048]{3,2,1,0:T(8,128)(2,1)S(1)} %copy-done.1), custom_call_target="tpu_custom_call" | custom-call | tf_op jit(solution)/shard_map/pack_body/pallas_call | solution.py:244
  1.7 7.5 %all-to-all-start = ((bf16[16,96,128]{2,1,0:T(8,128)(2,1)}), bf16[16,96,128]{2,1,0:T(8,128)(2,1)S(1)}, u32[]{:S(2)}, u32[]{:S(2)}) async-start(bf16[16,96,128]{2,1,0:T(8,128)(2,1)} %pack_body.1), calls=%async_computation | async-start | bytes 786432 | tf_op jit(solution)/shard_map/all_to_all | solution.py:268
  9.3 0.6 %cross_body.1 = f32[1,16,128]{2,1,0:T(8,128)S(1)} custom-call(bf16[3,2,8,2048]{3,2,1,0:T(8,128)(2,1)S(1)} %copy-done.2, bf16[3,2,32,2048]{3,2,1,0:T(8,128)(2,1)S(1)} %copy-done), custom_call_target="tpu_custom_call" | custom-call | flops 100000000 | bytes 1000000 | tf_op jit(solution)/shard_map/cross_body/pallas_call | solution.py:244
  9.8 0.4 %collective-permute-start = (f32[1,16,128]{2,1,0:T(8,128)S(1)}, f32[1,16,128]{2,1,0:T(8,128)S(1)}, u32[]{:S(2)}, u32[]{:S(2)}) collective-permute-start(f32[1,16,128]{2,1,0:T(8,128)S(1)} %cross_body.1), channel_id=1, source_target_pairs={{0,2},{2,0},{4,6},{6,4},{8,10},{10,8},{12,14},{14,12},{16,18},{18,... | collective-permute-start | bytes 24584 | tf_op jit(solution)/shard_map/hop/ppermute | solution.py:235
  10.3 0.8 %collective-permute-done = f32[1,16,128]{2,1,0:T(8,128)S(1)} collective-permute-done((f32[1,16,128]{2,1,0:T(8,128)S(1)}, f32[1,16,128]{2,1,0:T(8,128)S(1)}, u32[]{:S(2)}, u32[]{:S(2)}) %collective-permute-start) | collective-permute-done | bytes 8224 | tf_op jit(solution)/shard_map/hop/ppermute | solution.py:235
  11.1 1.9 %collective-permute-start.1 = (f32[2,16,128]{2,1,0:T(8,128)S(1)}, f32[2,16,128]{2,1,0:T(8,128)S(1)}, u32[]{:S(2)}, u32[]{:S(2)}) collective-permute-start(f32[2,16,128]{2,1,0:T(8,128)S(1)} %pad_maximum_fusion.3), channel_id=1, source_target_pairs={{0,4},{2,6},{4,0},{6,2},{8,12},{10,14},{12,8},{14,10},{16,20},{18,... | collective-permute-start | bytes 49160 | tf_op jit(solution)/shard_map/hop/ppermute | solution.py:235
  13.0 2.1 %system_body.1.system_ref = f32[2,3,32,40]{3,2,1,0:T(8,128)S(1)} custom-call(bf16[3,2,8,2048]{3,2,1,0:T(8,128)(2,1)S(1)} %copy-done.2, bf16[3,2,32,2048]{3,2,1,0:T(8,128)(2,1)S(1)} %copy-done), custom_call_target="tpu_custom_call" | custom-call | flops 1000000000 | bytes 20000000 | tf_op jit(solution)/shard_map/system_body/pallas_call | solution.py:244
  15.1 0.0 collective-permute-done.1
  15.1 1.6 %collective-permute-start.2 = (f32[4,16,128]{2,1,0:T(8,128)S(1)}, f32[4,16,128]{2,1,0:T(8,128)S(1)}, u32[]{:S(2)}, u32[]{:S(2)}) collective-permute-start(f32[4,16,128]{2,1,0:T(8,128)S(1)} %pad_maximum_fusion.2), channel_id=1, source_target_pairs={{0,8},{2,10},{4,12},{6,14},{8,0},{10,2},{12,4},{14,6},{16,24},{18,... | collective-permute-start | bytes 98312 | tf_op jit(solution)/shard_map/hop/ppermute | solution.py:235
  16.7 1.6 %solve_body.1.solved_ref = f32[3,2,32,8]{3,2,1,0:T(8,128)S(1)} custom-call(f32[2,3,32,40]{3,2,1,0:T(8,128)S(1)} %system_body.1.system_ref), custom_call_target="tpu_custom_call" | custom-call | flops 1000000000 | bytes 20000000 | tf_op jit(solution)/shard_map/solve_body/pallas_call | solution.py:244
  18.3 1.0 %collective-permute-done.2 = f32[4,16,128]{2,1,0:T(8,128)S(1)} collective-permute-done((f32[4,16,128]{2,1,0:T(8,128)S(1)}, f32[4,16,128]{2,1,0:T(8,128)S(1)}, u32[]{:S(2)}, u32[]{:S(2)}) %collective-permute-start.2) | collective-permute-done | bytes 32800 | tf_op jit(solution)/shard_map/hop/ppermute | solution.py:235
  19.3 2.5 %all-to-all-done.message_ref = bf16[16,96,128]{2,1,0:T(8,128)(2,1)S(1)} async-done(((bf16[16,96,128]{2,1,0:T(8,128)(2,1)}), bf16[16,96,128]{2,1,0:T(8,128)(2,1)S(1)}, u32[]{:S(2)}, u32[]{:S(2)}) %all-to-all-start) | async-done | bytes 393248 | tf_op jit(solution)/shard_map/all_to_all | solution.py:268
  21.9 0.3 product_body.1
  22.1 0.1 collective-permute-start.3
  22.2 1.3 %collective-permute-start.7 = (f32[8,16,128]{2,1,0:T(8,128)S(1)}, f32[8,16,128]{2,1,0:T(8,128)S(1)}, u32[]{:S(2)}, u32[]{:S(2)}) collective-permute-start(f32[8,16,128]{2,1,0:T(8,128)S(1)} %pad_maximum_fusion.1), channel_id=1, source_target_pairs={{0,16},{2,18},{4,20},{6,22},{8,24},{10,26},{12,28},{14,30},{16,0},... | collective-permute-start | bytes 196616 | tf_op jit(solution)/shard_map/last_hop/ppermute | solution.py:235
  23.6 0.2 collective-permute-start.4
  23.8 1.8 %collective-permute-start.5 = (f32[1,48,128]{2,1,0:T(8,128)S(1)}, f32[1,48,128]{2,1,0:T(8,128)S(1)}, u32[]{:S(2)}, u32[]{:S(2)}) collective-permute-start(f32[1,48,128]{2,1,0:T(8,128)S(1)} %get-tuple-element.18), channel_id=1, source_target_pairs={{0,8},{2,10},{4,12},{6,14},{8,0},{10,2},{12,4},{14,6},{16,24},{18,... | collective-permute-start | bytes 73736 | tf_op jit(solution)/shard_map/ppermute | solution.py:235
  25.6 1.6 %collective-permute-start.6 = (f32[1,48,128]{2,1,0:T(8,128)S(1)}, f32[1,48,128]{2,1,0:T(8,128)S(1)}, u32[]{:S(2)}, u32[]{:S(2)}) collective-permute-start(f32[1,48,128]{2,1,0:T(8,128)S(1)} %get-tuple-element.17), channel_id=1, source_target_pairs={{0,12},{2,14},{4,8},{6,10},{8,4},{10,6},{12,0},{14,2},{16,28},{18,... | collective-permute-start | bytes 73736 | tf_op jit(solution)/shard_map/ppermute | solution.py:235
  27.1 1.8 %collective-permute-done.7 = f32[8,16,128]{2,1,0:T(8,128)S(1)} collective-permute-done((f32[8,16,128]{2,1,0:T(8,128)S(1)}, f32[8,16,128]{2,1,0:T(8,128)S(1)}, u32[]{:S(2)}, u32[]{:S(2)}) %collective-permute-start.7) | collective-permute-done | bytes 65568 | tf_op jit(solution)/shard_map/last_hop/ppermute | solution.py:235
  28.9 0.4 %correction_body.1.refs_3_ = f32[3,2,8,128]{3,2,1,0:T(8,128)S(1)} custom-call(f32[16,16,128]{2,1,0:T(8,128)S(1)} %pad_maximum_fusion.cross_ref, f32[3,2,32,8]{3,2,1,0:T(8,128)S(1)} %solve_body.1.solved_ref), custom_call_target="tpu_custom_call" | custom-call | flops 100000000 | bytes 2000000 | tf_op jit(solution)/shard_map/correction_body/pallas_call | solution.py:244
  29.4 0.0 collective-permute-done.5.refs_1_
  29.4 0.9 %collective-permute-done.6.refs_2_ = f32[1,48,128]{2,1,0:T(8,128)S(1)} collective-permute-done((f32[1,48,128]{2,1,0:T(8,128)S(1)}, f32[1,48,128]{2,1,0:T(8,128)S(1)}, u32[]{:S(2)}, u32[]{:S(2)}) %collective-permute-start.6) | collective-permute-done | bytes 24608 | tf_op jit(solution)/shard_map/ppermute | solution.py:235
  30.3 0.6 %finish_body.1 = f32[3,2,8,128]{3,2,1,0:T(8,128)} custom-call(f32[1,48,128]{2,1,0:T(8,128)S(1)} %get-tuple-element.20.kept_ref, f32[1,48,128]{2,1,0:T(8,128)S(1)} %collective-permute-done.4.refs_0_, f32[1,48,128]{2,1,0:T(8,128)S(1)} %collective-permute-done.5.refs_1_, f32[1,48,128]{2,1,0:T(8,128)S(1)} %collective-permute-done.6.refs_2_, ...), custom_call_target="tpu_custom_call" | custom-call | tf_op jit(solution)/shard_map/finish_body/pallas_call | solution.py:244
  (13 shorter events, 0.1 us)
Async XLA Ops:
  0.0 0.9 %copy-start.1 = (bf16[3,2,8,2048]{3,2,1,0:T(8,128)(2,1)S(1)}, bf16[3,2,8,2048]{3,2,1,0:T(8,128)(2,1)}, u32[]{:S(2)}) copy-start(bf16[3,2,8,2048]{3,2,1,0:T(8,128)(2,1)} %volts_ref.5) | copy-start | bytes 589828
  0.9 8.3 %copy-start = (bf16[3,2,32,2048]{3,2,1,0:T(8,128)(2,1)S(1)}, bf16[3,2,32,2048]{3,2,1,0:T(8,128)(2,1)}, u32[]{:S(2)}) copy-start(bf16[3,2,32,2048]{3,2,1,0:T(8,128)(2,1)} %reference_ref.3) | copy-start | bytes 2359300
  1.7 7.5 %copy-start.2 = (bf16[3,2,8,2048]{3,2,1,0:T(8,128)(2,1)S(1)}, bf16[3,2,8,2048]{3,2,1,0:T(8,128)(2,1)}, u32[]{:S(2)}) copy-start(bf16[3,2,8,2048]{3,2,1,0:T(8,128)(2,1)} %volts_ref.5) | copy-start | bytes 589828
  1.7 20.1 %all-to-all-start = ((bf16[16,96,128]{2,1,0:T(8,128)(2,1)}), bf16[16,96,128]{2,1,0:T(8,128)(2,1)S(1)}, u32[]{:S(2)}, u32[]{:S(2)}) async-start(bf16[16,96,128]{2,1,0:T(8,128)(2,1)} %pack_body.1), calls=%async_computation | async-start | bytes 786432 | tf_op jit(solution)/shard_map/all_to_all | solution.py:268
  9.8 1.2 %collective-permute-start = (f32[1,16,128]{2,1,0:T(8,128)S(1)}, f32[1,16,128]{2,1,0:T(8,128)S(1)}, u32[]{:S(2)}, u32[]{:S(2)}) collective-permute-start(f32[1,16,128]{2,1,0:T(8,128)S(1)} %cross_body.1), channel_id=1, source_target_pairs={{0,2},{2,0},{4,6},{6,4},{8,10},{10,8},{12,14},{14,12},{16,18},{18,... | collective-permute-start | bytes 24584 | tf_op jit(solution)/shard_map/hop/ppermute | solution.py:235
  11.1 4.0 %collective-permute-start.1 = (f32[2,16,128]{2,1,0:T(8,128)S(1)}, f32[2,16,128]{2,1,0:T(8,128)S(1)}, u32[]{:S(2)}, u32[]{:S(2)}) collective-permute-start(f32[2,16,128]{2,1,0:T(8,128)S(1)} %pad_maximum_fusion.3), channel_id=1, source_target_pairs={{0,4},{2,6},{4,0},{6,2},{8,12},{10,14},{12,8},{14,10},{16,20},{18,... | collective-permute-start | bytes 49160 | tf_op jit(solution)/shard_map/hop/ppermute | solution.py:235
  15.1 4.2 %collective-permute-start.2 = (f32[4,16,128]{2,1,0:T(8,128)S(1)}, f32[4,16,128]{2,1,0:T(8,128)S(1)}, u32[]{:S(2)}, u32[]{:S(2)}) collective-permute-start(f32[4,16,128]{2,1,0:T(8,128)S(1)} %pad_maximum_fusion.2), channel_id=1, source_target_pairs={{0,8},{2,10},{4,12},{6,14},{8,0},{10,2},{12,4},{14,6},{16,24},{18,... | collective-permute-start | bytes 98312 | tf_op jit(solution)/shard_map/hop/ppermute | solution.py:235
  22.1 1.4 %collective-permute-start.3 = (f32[4,48,128]{2,1,0:T(8,128)S(1)}, f32[4,48,128]{2,1,0:T(8,128)S(1)}, u32[]{:S(2)}, u32[]{:S(2)}) collective-permute-start(f32[4,48,128]{2,1,0:T(8,128)S(1)} %get-tuple-element.14), channel_id=1, source_target_pairs={{0,2},{2,0},{4,6},{6,4},{8,10},{10,8},{12,14},{14,12},{16,18},{18,... | collective-permute-start | bytes 294920 | tf_op jit(solution)/shard_map/ppermute | solution.py:235
  22.2 6.7 %collective-permute-start.7 = (f32[8,16,128]{2,1,0:T(8,128)S(1)}, f32[8,16,128]{2,1,0:T(8,128)S(1)}, u32[]{:S(2)}, u32[]{:S(2)}) collective-permute-start(f32[8,16,128]{2,1,0:T(8,128)S(1)} %pad_maximum_fusion.1), channel_id=1, source_target_pairs={{0,16},{2,18},{4,20},{6,22},{8,24},{10,26},{12,28},{14,30},{16,0},... | collective-permute-start | bytes 196616 | tf_op jit(solution)/shard_map/last_hop/ppermute | solution.py:235
  23.6 5.8 %collective-permute-start.4 = (f32[1,48,128]{2,1,0:T(8,128)S(1)}, f32[1,48,128]{2,1,0:T(8,128)S(1)}, u32[]{:S(2)}, u32[]{:S(2)}) collective-permute-start(f32[1,48,128]{2,1,0:T(8,128)S(1)} %get-tuple-element.19), channel_id=1, source_target_pairs={{0,4},{2,6},{4,0},{6,2},{8,12},{10,14},{12,8},{14,10},{16,20},{18,... | collective-permute-start | bytes 73736 | tf_op jit(solution)/shard_map/ppermute | solution.py:235
  23.8 5.6 %collective-permute-start.5 = (f32[1,48,128]{2,1,0:T(8,128)S(1)}, f32[1,48,128]{2,1,0:T(8,128)S(1)}, u32[]{:S(2)}, u32[]{:S(2)}) collective-permute-start(f32[1,48,128]{2,1,0:T(8,128)S(1)} %get-tuple-element.18), channel_id=1, source_target_pairs={{0,8},{2,10},{4,12},{6,14},{8,0},{10,2},{12,4},{14,6},{16,24},{18,... | collective-permute-start | bytes 73736 | tf_op jit(solution)/shard_map/ppermute | solution.py:235
  25.6 4.7 %collective-permute-start.6 = (f32[1,48,128]{2,1,0:T(8,128)S(1)}, f32[1,48,128]{2,1,0:T(8,128)S(1)}, u32[]{:S(2)}, u32[]{:S(2)}) collective-permute-start(f32[1,48,128]{2,1,0:T(8,128)S(1)} %get-tuple-element.17), channel_id=1, source_target_pairs={{0,12},{2,14},{4,8},{6,10},{8,4},{10,6},{12,0},{14,2},{16,28},{18,... | collective-permute-start | bytes 73736 | tf_op jit(solution)/shard_map/ppermute | solution.py:235

commit v4 on v3

--- a/solution.py
+++ b/solution.py
@@ -311,7 +311,8 @@
         ants=ants,
     )
     sums = even + swap(odd, 1, n_row)
-    parts = [sums[:1]] + [swap(sums[k : k + 1], 2 * k, n_row) for k in range(1, group // 2)]
+    parts = [swap(sums[k : k + 1], 2 * k, n_row) for k in range(group // 2 - 1, 0, -1)]
+    parts.append(sums[:1])
     correction = call(
         correction_body,
         pltpu.VMEM((subs, 2, ants, n_row * ants), f32),

time: 31.1 us -> 30.2 us (0.971)
  waiting for transfers between devices: 7.12 us -> 6.13 us
    ppermute x8, waiting for transfers between devices: 4.59 us -> 3.6 us  [swap(): return lax.ppermute(x, 'row', [(i, i ^ bit) for i in range(n_row)])]
  transfers between devices with their start and end apart: 9 -> 9, of which waited for: 5 -> 4; matrix products, arithmetic and copies ran while one was open for 0% -> 0% of each run, Pallas kernels for 15% -> 16%
where the time goes in v4:
time: 30.2 us; the launch traced here: 29.9 us
  starting transfers between devices  16.3 us (54%)
  Pallas kernels  6.38 us (21%)
  waiting for transfers between devices  6.13 us (20%)
  local copies, waits for them, and re-layouts  0.94 us (3%)
    ppermute x8, starting transfers between devices, swap(): return lax.ppermute(x, 'row', [(i, i ^ bit) for i in range(n_row)])  8.82 us
    all_to_all x1, starting transfers between devices, per_device(): lax.all_to_all(message, 'row', split_axis=0, concat_axis=0, tiled=True)  7.52 us
    pallas_call x7, Pallas kernels, call(): pl.pallas_call(functools.partial(body, **kw) if kw else body, out_shape=o...  6.38 us
    ppermute x8, waiting for transfers between devices, swap(): return lax.ppermute(x, 'row', [(i, i ^ bit) for i in range(n_row)])  3.6 us
    all_to_all x1, waiting for transfers between devices, per_device(): lax.all_to_all(message, 'row', split_axis=0, concat_axis=0, tiled=True)  2.53 us
    unnamed x6, local copies, waits for them, and re-layouts  0.93 us
  transfers between devices with their start and end apart: 9, of which 4 were waited for; matrix products, arithmetic and copies ran while one was open for 0% of the time, Pallas kernels for 16%

profile of v4, /device:TPU:0, one launch (start us, length us, event | category | flops | bytes accessed | tf_op | source)
XLA Modules:
  0.0 29.9 jit_solution(6971675329726705566)
XLA Ops:
  0.0 0.9 %copy-done.1 = bf16[3,2,8,2048]{3,2,1,0:T(8,128)(2,1)S(1)} copy-done((bf16[3,2,8,2048]{3,2,1,0:T(8,128)(2,1)S(1)}, bf16[3,2,8,2048]{3,2,1,0:T(8,128)(2,1)}, u32[]{:S(2)}) %copy-start.1) | copy-done | bytes 196632
  0.9 0.8 %pack_body.1 = bf16[16,96,128]{2,1,0:T(8,128)(2,1)} custom-call(bf16[3,2,8,2048]{3,2,1,0:T(8,128)(2,1)S(1)} %copy-done.1), custom_call_target="tpu_custom_call" | custom-call | tf_op jit(solution)/shard_map/pack_body/pallas_call | solution.py:244
  1.7 7.5 %all-to-all-start = ((bf16[16,96,128]{2,1,0:T(8,128)(2,1)}), bf16[16,96,128]{2,1,0:T(8,128)(2,1)S(1)}, u32[]{:S(2)}, u32[]{:S(2)}) async-start(bf16[16,96,128]{2,1,0:T(8,128)(2,1)} %pack_body.1), calls=%async_computation | async-start | bytes 786432 | tf_op jit(solution)/shard_map/all_to_all | solution.py:268
  9.3 0.6 %cross_body.1 = f32[1,16,128]{2,1,0:T(8,128)S(1)} custom-call(bf16[3,2,8,2048]{3,2,1,0:T(8,128)(2,1)S(1)} %copy-done.2, bf16[3,2,32,2048]{3,2,1,0:T(8,128)(2,1)S(1)} %copy-done), custom_call_target="tpu_custom_call" | custom-call | flops 100000000 | bytes 1000000 | tf_op jit(solution)/shard_map/cross_body/pallas_call | solution.py:244
  9.8 0.4 %collective-permute-start = (f32[1,16,128]{2,1,0:T(8,128)S(1)}, f32[1,16,128]{2,1,0:T(8,128)S(1)}, u32[]{:S(2)}, u32[]{:S(2)}) collective-permute-start(f32[1,16,128]{2,1,0:T(8,128)S(1)} %cross_body.1), channel_id=1, source_target_pairs={{0,2},{2,0},{4,6},{6,4},{8,10},{10,8},{12,14},{14,12},{16,18},{18,... | collective-permute-start | bytes 24584 | tf_op jit(solution)/shard_map/hop/ppermute | solution.py:235
  10.3 0.8 %collective-permute-done = f32[1,16,128]{2,1,0:T(8,128)S(1)} collective-permute-done((f32[1,16,128]{2,1,0:T(8,128)S(1)}, f32[1,16,128]{2,1,0:T(8,128)S(1)}, u32[]{:S(2)}, u32[]{:S(2)}) %collective-permute-start) | collective-permute-done | bytes 8224 | tf_op jit(solution)/shard_map/hop/ppermute | solution.py:235
  11.1 1.9 %collective-permute-start.1 = (f32[2,16,128]{2,1,0:T(8,128)S(1)}, f32[2,16,128]{2,1,0:T(8,128)S(1)}, u32[]{:S(2)}, u32[]{:S(2)}) collective-permute-start(f32[2,16,128]{2,1,0:T(8,128)S(1)} %pad_maximum_fusion.3), channel_id=1, source_target_pairs={{0,4},{2,6},{4,0},{6,2},{8,12},{10,14},{12,8},{14,10},{16,20},{18,... | collective-permute-start | bytes 49160 | tf_op jit(solution)/shard_map/hop/ppermute | solution.py:235
  13.0 2.1 %system_body.1.system_ref = f32[2,3,32,40]{3,2,1,0:T(8,128)S(1)} custom-call(bf16[3,2,8,2048]{3,2,1,0:T(8,128)(2,1)S(1)} %copy-done.2, bf16[3,2,32,2048]{3,2,1,0:T(8,128)(2,1)S(1)} %copy-done), custom_call_target="tpu_custom_call" | custom-call | flops 1000000000 | bytes 20000000 | tf_op jit(solution)/shard_map/system_body/pallas_call | solution.py:244
  15.1 0.0 collective-permute-done.1
  15.1 1.6 %collective-permute-start.2 = (f32[4,16,128]{2,1,0:T(8,128)S(1)}, f32[4,16,128]{2,1,0:T(8,128)S(1)}, u32[]{:S(2)}, u32[]{:S(2)}) collective-permute-start(f32[4,16,128]{2,1,0:T(8,128)S(1)} %pad_maximum_fusion.2), channel_id=1, source_target_pairs={{0,8},{2,10},{4,12},{6,14},{8,0},{10,2},{12,4},{14,6},{16,24},{18,... | collective-permute-start | bytes 98312 | tf_op jit(solution)/shard_map/hop/ppermute | solution.py:235
  16.7 1.6 %solve_body.1.solved_ref = f32[3,2,32,8]{3,2,1,0:T(8,128)S(1)} custom-call(f32[2,3,32,40]{3,2,1,0:T(8,128)S(1)} %system_body.1.system_ref), custom_call_target="tpu_custom_call" | custom-call | flops 1000000000 | bytes 20000000 | tf_op jit(solution)/shard_map/solve_body/pallas_call | solution.py:244
  18.3 1.0 %collective-permute-done.2 = f32[4,16,128]{2,1,0:T(8,128)S(1)} collective-permute-done((f32[4,16,128]{2,1,0:T(8,128)S(1)}, f32[4,16,128]{2,1,0:T(8,128)S(1)}, u32[]{:S(2)}, u32[]{:S(2)}) %collective-permute-start.2) | collective-permute-done | bytes 32800 | tf_op jit(solution)/shard_map/hop/ppermute | solution.py:235
  19.3 2.5 %all-to-all-done.message_ref = bf16[16,96,128]{2,1,0:T(8,128)(2,1)S(1)} async-done(((bf16[16,96,128]{2,1,0:T(8,128)(2,1)}), bf16[16,96,128]{2,1,0:T(8,128)(2,1)S(1)}, u32[]{:S(2)}, u32[]{:S(2)}) %all-to-all-start) | async-done | bytes 393248 | tf_op jit(solution)/shard_map/all_to_all | solution.py:268
  21.9 0.3 product_body.1
  22.1 0.1 collective-permute-start.3
  22.2 1.3 %collective-permute-start.7 = (f32[8,16,128]{2,1,0:T(8,128)S(1)}, f32[8,16,128]{2,1,0:T(8,128)S(1)}, u32[]{:S(2)}, u32[]{:S(2)}) collective-permute-start(f32[8,16,128]{2,1,0:T(8,128)S(1)} %pad_maximum_fusion.1), channel_id=1, source_target_pairs={{0,16},{2,18},{4,20},{6,22},{8,24},{10,26},{12,28},{14,30},{16,0},... | collective-permute-start | bytes 196616 | tf_op jit(solution)/shard_map/last_hop/ppermute | solution.py:235
  23.5 0.0 collective-permute-done.3
  23.6 1.4 %collective-permute-start.4 = (f32[1,48,128]{2,1,0:T(8,128)S(1)}, f32[1,48,128]{2,1,0:T(8,128)S(1)}, u32[]{:S(2)}, u32[]{:S(2)}) collective-permute-start(f32[1,48,128]{2,1,0:T(8,128)S(1)} %get-tuple-element.20), channel_id=1, source_target_pairs={{0,12},{2,14},{4,8},{6,10},{8,4},{10,6},{12,0},{14,2},{16,28},{18,... | collective-permute-start | bytes 73736 | tf_op jit(solution)/shard_map/ppermute | solution.py:235
  25.0 0.3 collective-permute-start.5
  25.3 1.9 %collective-permute-start.6 = (f32[1,48,128]{2,1,0:T(8,128)S(1)}, f32[1,48,128]{2,1,0:T(8,128)S(1)}, u32[]{:S(2)}, u32[]{:S(2)}) collective-permute-start(f32[1,48,128]{2,1,0:T(8,128)S(1)} %get-tuple-element.18), channel_id=1, source_target_pairs={{0,4},{2,6},{4,0},{6,2},{8,12},{10,14},{12,8},{14,10},{16,20},{18,... | collective-permute-start | bytes 73736 | tf_op jit(solution)/shard_map/ppermute | solution.py:235
  27.1 1.7 %collective-permute-done.7 = f32[8,16,128]{2,1,0:T(8,128)S(1)} collective-permute-done((f32[8,16,128]{2,1,0:T(8,128)S(1)}, f32[8,16,128]{2,1,0:T(8,128)S(1)}, u32[]{:S(2)}, u32[]{:S(2)}) %collective-permute-start.7) | collective-permute-done | bytes 65568 | tf_op jit(solution)/shard_map/last_hop/ppermute | solution.py:235
  28.9 0.4 %correction_body.1.refs_3_ = f32[3,2,8,128]{3,2,1,0:T(8,128)S(1)} custom-call(f32[16,16,128]{2,1,0:T(8,128)S(1)} %pad_maximum_fusion.cross_ref, f32[3,2,32,8]{3,2,1,0:T(8,128)S(1)} %solve_body.1.solved_ref), custom_call_target="tpu_custom_call" | custom-call | flops 100000000 | bytes 2000000 | tf_op jit(solution)/shard_map/correction_body/pallas_call | solution.py:244
  29.3 0.0 collective-permute-done.5.refs_0_
  29.3 0.6 %finish_body.1 = f32[3,2,8,128]{3,2,1,0:T(8,128)} custom-call(f32[1,48,128]{2,1,0:T(8,128)S(1)} %collective-permute-done.4.kept_ref, f32[1,48,128]{2,1,0:T(8,128)S(1)} %collective-permute-done.5.refs_0_, f32[1,48,128]{2,1,0:T(8,128)S(1)} %collective-permute-done.6.refs_1_, f32[1,48,128]{2,1,0:T(8,128)S(1)} %get-tuple-element.17.refs_2_, ...), custom_call_target="tpu_custom_call" | custom-call | tf_op jit(solution)/shard_map/finish_body/pallas_call | solution.py:244
  (13 shorter events, 0.1 us)
Async XLA Ops:
  0.0 0.9 %copy-start.1 = (bf16[3,2,8,2048]{3,2,1,0:T(8,128)(2,1)S(1)}, bf16[3,2,8,2048]{3,2,1,0:T(8,128)(2,1)}, u32[]{:S(2)}) copy-start(bf16[3,2,8,2048]{3,2,1,0:T(8,128)(2,1)} %volts_ref.5) | copy-start | bytes 589828
  0.9 8.3 %copy-start = (bf16[3,2,32,2048]{3,2,1,0:T(8,128)(2,1)S(1)}, bf16[3,2,32,2048]{3,2,1,0:T(8,128)(2,1)}, u32[]{:S(2)}) copy-start(bf16[3,2,32,2048]{3,2,1,0:T(8,128)(2,1)} %reference_ref.3) | copy-start | bytes 2359300
  1.7 7.5 %copy-start.2 = (bf16[3,2,8,2048]{3,2,1,0:T(8,128)(2,1)S(1)}, bf16[3,2,8,2048]{3,2,1,0:T(8,128)(2,1)}, u32[]{:S(2)}) copy-start(bf16[3,2,8,2048]{3,2,1,0:T(8,128)(2,1)} %volts_ref.5) | copy-start | bytes 589828
  1.7 20.1 %all-to-all-start = ((bf16[16,96,128]{2,1,0:T(8,128)(2,1)}), bf16[16,96,128]{2,1,0:T(8,128)(2,1)S(1)}, u32[]{:S(2)}, u32[]{:S(2)}) async-start(bf16[16,96,128]{2,1,0:T(8,128)(2,1)} %pack_body.1), calls=%async_computation | async-start | bytes 786432 | tf_op jit(solution)/shard_map/all_to_all | solution.py:268
  9.8 1.2 %collective-permute-start = (f32[1,16,128]{2,1,0:T(8,128)S(1)}, f32[1,16,128]{2,1,0:T(8,128)S(1)}, u32[]{:S(2)}, u32[]{:S(2)}) collective-permute-start(f32[1,16,128]{2,1,0:T(8,128)S(1)} %cross_body.1), channel_id=1, source_target_pairs={{0,2},{2,0},{4,6},{6,4},{8,10},{10,8},{12,14},{14,12},{16,18},{18,... | collective-permute-start | bytes 24584 | tf_op jit(solution)/shard_map/hop/ppermute | solution.py:235
  11.1 4.0 %collective-permute-start.1 = (f32[2,16,128]{2,1,0:T(8,128)S(1)}, f32[2,16,128]{2,1,0:T(8,128)S(1)}, u32[]{:S(2)}, u32[]{:S(2)}) collective-permute-start(f32[2,16,128]{2,1,0:T(8,128)S(1)} %pad_maximum_fusion.3), channel_id=1, source_target_pairs={{0,4},{2,6},{4,0},{6,2},{8,12},{10,14},{12,8},{14,10},{16,20},{18,... | collective-permute-start | bytes 49160 | tf_op jit(solution)/shard_map/hop/ppermute | solution.py:235
  15.1 4.2 %collective-permute-start.2 = (f32[4,16,128]{2,1,0:T(8,128)S(1)}, f32[4,16,128]{2,1,0:T(8,128)S(1)}, u32[]{:S(2)}, u32[]{:S(2)}) collective-permute-start(f32[4,16,128]{2,1,0:T(8,128)S(1)} %pad_maximum_fusion.2), channel_id=1, source_target_pairs={{0,8},{2,10},{4,12},{6,14},{8,0},{10,2},{12,4},{14,6},{16,24},{18,... | collective-permute-start | bytes 98312 | tf_op jit(solution)/shard_map/hop/ppermute | solution.py:235
  22.1 1.4 %collective-permute-start.3 = (f32[4,48,128]{2,1,0:T(8,128)S(1)}, f32[4,48,128]{2,1,0:T(8,128)S(1)}, u32[]{:S(2)}, u32[]{:S(2)}) collective-permute-start(f32[4,48,128]{2,1,0:T(8,128)S(1)} %get-tuple-element.14), channel_id=1, source_target_pairs={{0,2},{2,0},{4,6},{6,4},{8,10},{10,8},{12,14},{14,12},{16,18},{18,... | collective-permute-start | bytes 294920 | tf_op jit(solution)/shard_map/ppermute | solution.py:235
  22.2 6.6 %collective-permute-start.7 = (f32[8,16,128]{2,1,0:T(8,128)S(1)}, f32[8,16,128]{2,1,0:T(8,128)S(1)}, u32[]{:S(2)}, u32[]{:S(2)}) collective-permute-start(f32[8,16,128]{2,1,0:T(8,128)S(1)} %pad_maximum_fusion.1), channel_id=1, source_target_pairs={{0,16},{2,18},{4,20},{6,22},{8,24},{10,26},{12,28},{14,30},{16,0},... | collective-permute-start | bytes 196616 | tf_op jit(solution)/shard_map/last_hop/ppermute | solution.py:235
  23.6 5.7 %collective-permute-start.4 = (f32[1,48,128]{2,1,0:T(8,128)S(1)}, f32[1,48,128]{2,1,0:T(8,128)S(1)}, u32[]{:S(2)}, u32[]{:S(2)}) collective-permute-start(f32[1,48,128]{2,1,0:T(8,128)S(1)} %get-tuple-element.20), channel_id=1, source_target_pairs={{0,12},{2,14},{4,8},{6,10},{8,4},{10,6},{12,0},{14,2},{16,28},{18,... | collective-permute-start | bytes 73736 | tf_op jit(solution)/shard_map/ppermute | solution.py:235
  25.0 4.3 %collective-permute-start.5 = (f32[1,48,128]{2,1,0:T(8,128)S(1)}, f32[1,48,128]{2,1,0:T(8,128)S(1)}, u32[]{:S(2)}, u32[]{:S(2)}) collective-permute-start(f32[1,48,128]{2,1,0:T(8,128)S(1)} %get-tuple-element.19), channel_id=1, source_target_pairs={{0,8},{2,10},{4,12},{6,14},{8,0},{10,2},{12,4},{14,6},{16,24},{18,... | collective-permute-start | bytes 73736 | tf_op jit(solution)/shard_map/ppermute | solution.py:235
  25.3 4.0 %collective-permute-start.6 = (f32[1,48,128]{2,1,0:T(8,128)S(1)}, f32[1,48,128]{2,1,0:T(8,128)S(1)}, u32[]{:S(2)}, u32[]{:S(2)}) collective-permute-start(f32[1,48,128]{2,1,0:T(8,128)S(1)} %get-tuple-element.18), channel_id=1, source_target_pairs={{0,4},{2,6},{4,0},{6,2},{8,12},{10,14},{12,8},{14,10},{16,20},{18,... | collective-permute-start | bytes 73736 | tf_op jit(solution)/shard_map/ppermute | solution.py:235

commit v5 on v4

--- a/solution.py
+++ b/solution.py
@@ -187,35 +187,55 @@
 
 def correction_body(cross_ref, solved_ref, correction_ref):
     subs, _, nref, ants = solved_ref.shape
+    count = correction_ref.shape[3] // ants
+    whole = subs // 2 * ants
     me = lax.axis_index("row")
-    for pair in range((subs + 1) // 2):
-        members = range(2 * pair, min(2 * pair + 2, subs))
-        cross = jnp.concatenate(
-            [
-                cross_ref[me ^ m, pair * ants : (pair + 1) * ants, :]
-                for m in range(cross_ref.shape[0])
-            ],
-            0,
-        )
-        columns = []
-        for s in members:
-            re, im = solved_ref[s, 0], solved_ref[s, 1]
-            none = jnp.zeros((2 * nref, ants), jnp.float32)
-            for stack in ([re, -im], [-im, -re]):
-                columns.append(
-                    jnp.concatenate(stack + [none] if s % 2 == 0 else [none] + stack, 0)
-                )
-        out = lax.dot_general(
+    none = jnp.zeros((2 * nref, ants), jnp.float32)
+
+    def product(columns, cross):
+        return lax.dot_general(
             jnp.concatenate(columns, 1),
             cross,
             TT,
             precision=HIGHEST,
             preferred_element_type=jnp.float32,
         )
-        for k, s in enumerate(members):
+
+    def stacks(s):
+        re, im = solved_ref[s, 0], solved_ref[s, 1]
+        return [re, -im], [-im, -re]
+
+    for first in range(0, subs - 1, 2):
+        cross = jnp.concatenate(
+            [
+                cross_ref[
+                    (me ^ m) // 2,
+                    pl.ds(pl.multiple_of((me ^ m) % 2 * whole + first // 2 * ants, 8), ants),
+                    :,
+                ]
+                for m in range(count)
+            ],
+            0,
+        )
+        columns = [jnp.concatenate(stack + [none], 0) for stack in stacks(first)]
+        columns += [jnp.concatenate([none] + stack, 0) for stack in stacks(first + 1)]
+        out = product(columns, cross)
+        for k in range(2):
             for p in range(2):
                 at = (2 * k + p) * ants
-                correction_ref[s, p] = out[at : at + ants]
+                correction_ref[first + k, p] = out[at : at + ants]
+    if subs % 2:
+        cross = jnp.concatenate(
+            [cross_ref[(me ^ m) // 2, 2 * whole : 2 * whole + ants, :] for m in range(count)], 0
+        )
+        columns = [jnp.concatenate(stack + [none], 0) for stack in stacks(subs - 1)]
+        columns += [jnp.concatenate([none] + stack, 0) for stack in stacks(subs - 1)]
+        out = product(columns, cross)
+        owner = lax.broadcasted_iota(jnp.int32, (ants, count * ants), 1) // ants
+        lower = (owner ^ me) % 2 == 0
+        for p in range(2):
+            low, high = out[p * ants : (p + 1) * ants], out[(2 + p) * ants : (3 + p) * ants]
+            correction_ref[subs - 1, p] = jnp.where(lower, low, high)
 
 
 def finish_body(kept_ref, *refs, samples):
@@ -229,6 +249,15 @@
         for p in range(2):
             at = (s * 2 + p) * ants
             cleaned_ref[s, p] = total[at : at + ants] - correction_ref[s, p]
+
+
+def chip(mine, partner, subs, ants):
+    whole = subs // 2 * ants
+    parts = [mine[:, :whole], partner[:, :whole]]
+    if subs % 2:
+        half = mine.shape[2] // 2
+        parts.append(jnp.concatenate([mine[:, whole:, :half], partner[:, whole:, :half]], 2))
+    return jnp.concatenate(parts, 1)
 
 
 def swap(x, bit, n_row):
@@ -281,7 +310,7 @@
             volts, crosses = lax.optimization_barrier((volts, crosses))
         with jax.named_scope("last_hop" if last else "hop"):
             other = swap(crosses, bit, n_row)
-        crosses = jnp.concatenate([crosses, other], 0)
+        crosses = jnp.concatenate([crosses, other], 0) if bit > 1 else chip(crosses, other, subs, ants)
         bit *= 2
     system = call(
         system_body,

time: 30.2 us -> 29.9 us (0.990)
  waiting for transfers between devices: 6.13 us -> 5.63 us
    ppermute x8, waiting for transfers between devices: 3.6 us -> 3.19 us  [swap(): return lax.ppermute(x, 'row', [(i, i ^ bit) for i in range(n_row)])]
  transfers between devices with their start and end apart: 9 -> 9, of which waited for: 4 -> 6; matrix products, arithmetic and copies ran while one was open for 0% -> 1% of each run, Pallas kernels for 16% -> 16%
where the time goes in v5:
time: 29.9 us; the launch traced here: 29.7 us
  starting transfers between devices  16.4 us (55%)
  Pallas kernels  6.41 us (21%)
  waiting for transfers between devices  5.63 us (19%)
  local copies, waits for them, and re-layouts  0.95 us (3%)
    ppermute x8, starting transfers between devices, swap(): return lax.ppermute(x, 'row', [(i, i ^ bit) for i in range(n_row)])  8.87 us
    all_to_all x1, starting transfers between devices, per_device(): lax.all_to_all(message, 'row', split_axis=0, concat_axis=0, tiled=True)  7.52 us
    pallas_call x7, Pallas kernels, call(): pl.pallas_call(functools.partial(body, **kw) if kw else body, out_shape=o...  6.41 us
    ppermute x8, waiting for transfers between devices, swap(): return lax.ppermute(x, 'row', [(i, i ^ bit) for i in range(n_row)])  3.19 us
    all_to_all x1, waiting for transfers between devices, per_device(): lax.all_to_all(message, 'row', split_axis=0, concat_axis=0, tiled=True)  2.44 us
    unnamed x6, local copies, waits for them, and re-layouts  0.93 us
  transfers between devices with their start and end apart: 9, of which 6 were waited for; matrix products, arithmetic and copies ran while one was open for 1% of the time, Pallas kernels for 16%

profile of v5, /device:TPU:0, one launch (start us, length us, event | category | flops | bytes accessed | tf_op | source)
XLA Modules:
  0.0 29.7 jit_solution(2698397511483743181)
XLA Ops:
  0.0 0.9 %copy-done.1 = bf16[3,2,8,2048]{3,2,1,0:T(8,128)(2,1)S(1)} copy-done((bf16[3,2,8,2048]{3,2,1,0:T(8,128)(2,1)S(1)}, bf16[3,2,8,2048]{3,2,1,0:T(8,128)(2,1)}, u32[]{:S(2)}) %copy-start.1) | copy-done | bytes 196632
  0.9 0.8 %pack_body.1 = bf16[16,96,128]{2,1,0:T(8,128)(2,1)} custom-call(bf16[3,2,8,2048]{3,2,1,0:T(8,128)(2,1)S(1)} %copy-done.1), custom_call_target="tpu_custom_call" | custom-call | tf_op jit(solution)/shard_map/pack_body/pallas_call | solution.py:273
  1.7 7.5 %all-to-all-start = ((bf16[16,96,128]{2,1,0:T(8,128)(2,1)}), bf16[16,96,128]{2,1,0:T(8,128)(2,1)S(1)}, u32[]{:S(2)}, u32[]{:S(2)}) async-start(bf16[16,96,128]{2,1,0:T(8,128)(2,1)} %pack_body.1), calls=%async_computation | async-start | bytes 786432 | tf_op jit(solution)/shard_map/all_to_all | solution.py:297
  9.3 0.6 %cross_body.1 = f32[1,16,128]{2,1,0:T(8,128)S(1)} custom-call(bf16[3,2,8,2048]{3,2,1,0:T(8,128)(2,1)S(1)} %copy-done.2, bf16[3,2,32,2048]{3,2,1,0:T(8,128)(2,1)S(1)} %copy-done), custom_call_target="tpu_custom_call" | custom-call | flops 100000000 | bytes 1000000 | tf_op jit(solution)/shard_map/cross_body/pallas_call | solution.py:273
  9.8 0.4 %collective-permute-start = (f32[1,16,128]{2,1,0:T(8,128)S(1)}, f32[1,16,128]{2,1,0:T(8,128)S(1)}, u32[]{:S(2)}, u32[]{:S(2)}) collective-permute-start(f32[1,16,128]{2,1,0:T(8,128)S(1)} %cross_body.1), channel_id=1, source_target_pairs={{0,2},{2,0},{4,6},{6,4},{8,10},{10,8},{12,14},{14,12},{16,18},{18,... | collective-permute-start | bytes 24584 | tf_op jit(solution)/shard_map/hop/ppermute | solution.py:264
  10.3 0.8 %collective-permute-done = f32[1,16,128]{2,1,0:T(8,128)S(1)} collective-permute-done((f32[1,16,128]{2,1,0:T(8,128)S(1)}, f32[1,16,128]{2,1,0:T(8,128)S(1)}, u32[]{:S(2)}, u32[]{:S(2)}) %collective-permute-start) | collective-permute-done | bytes 8224 | tf_op jit(solution)/shard_map/hop/ppermute | solution.py:264
  11.1 0.1 maximum_maximum_fusion
  11.2 1.9 %collective-permute-start.1 = (f32[1,24,128]{2,1,0:T(8,128)S(1)}, f32[1,24,128]{2,1,0:T(8,128)S(1)}, u32[]{:S(2)}, u32[]{:S(2)}) collective-permute-start(f32[1,24,128]{2,1,0:T(8,128)S(1)} %maximum_maximum_fusion), channel_id=1, source_target_pairs={{0,4},{2,6},{4,0},{6,2},{8,12},{10,14},{12,8},{14,10},{16,20},{18,... | collective-permute-start | bytes 36872 | tf_op jit(solution)/shard_map/hop/ppermute | solution.py:264
  13.0 2.1 %system_body.1.system_ref = f32[2,3,32,40]{3,2,1,0:T(8,128)S(1)} custom-call(bf16[3,2,8,2048]{3,2,1,0:T(8,128)(2,1)S(1)} %copy-done.2, bf16[3,2,32,2048]{3,2,1,0:T(8,128)(2,1)S(1)} %copy-done), custom_call_target="tpu_custom_call" | custom-call | flops 1000000000 | bytes 20000000 | tf_op jit(solution)/shard_map/system_body/pallas_call | solution.py:273
  15.2 0.1 pad_maximum_fusion.2
  15.3 1.5 %collective-permute-start.2 = (f32[2,24,128]{2,1,0:T(8,128)S(1)}, f32[2,24,128]{2,1,0:T(8,128)S(1)}, u32[]{:S(2)}, u32[]{:S(2)}) collective-permute-start(f32[2,24,128]{2,1,0:T(8,128)S(1)} %pad_maximum_fusion.2), channel_id=1, source_target_pairs={{0,8},{2,10},{4,12},{6,14},{8,0},{10,2},{12,4},{14,6},{16,24},{18,... | collective-permute-start | bytes 73736 | tf_op jit(solution)/shard_map/hop/ppermute | solution.py:264
  16.8 1.6 %solve_body.1.solved_ref = f32[3,2,32,8]{3,2,1,0:T(8,128)S(1)} custom-call(f32[2,3,32,40]{3,2,1,0:T(8,128)S(1)} %system_body.1.system_ref), custom_call_target="tpu_custom_call" | custom-call | flops 1000000000 | bytes 20000000 | tf_op jit(solution)/shard_map/solve_body/pallas_call | solution.py:273
  18.4 0.9 %collective-permute-done.2 = f32[2,24,128]{2,1,0:T(8,128)S(1)} collective-permute-done((f32[2,24,128]{2,1,0:T(8,128)S(1)}, f32[2,24,128]{2,1,0:T(8,128)S(1)}, u32[]{:S(2)}, u32[]{:S(2)}) %collective-permute-start.2) | collective-permute-done | bytes 24608 | tf_op jit(solution)/shard_map/hop/ppermute | solution.py:264
  19.3 2.4 %all-to-all-done.message_ref = bf16[16,96,128]{2,1,0:T(8,128)(2,1)S(1)} async-done(((bf16[16,96,128]{2,1,0:T(8,128)(2,1)}), bf16[16,96,128]{2,1,0:T(8,128)(2,1)S(1)}, u32[]{:S(2)}, u32[]{:S(2)}) %all-to-all-start) | async-done | bytes 393248 | tf_op jit(solution)/shard_map/all_to_all | solution.py:297
  21.8 0.3 product_body.1
  22.1 1.4 %collective-permute-start.7 = (f32[4,24,128]{2,1,0:T(8,128)S(1)}, f32[4,24,128]{2,1,0:T(8,128)S(1)}, u32[]{:S(2)}, u32[]{:S(2)}) collective-permute-start(f32[4,24,128]{2,1,0:T(8,128)S(1)} %pad_maximum_fusion.1), channel_id=1, source_target_pairs={{0,16},{2,18},{4,20},{6,22},{8,24},{10,26},{12,28},{14,30},{16,0},... | collective-permute-start | bytes 147464 | tf_op jit(solution)/shard_map/last_hop/ppermute | solution.py:264
  23.6 1.4 %collective-permute-start.4 = (f32[1,48,128]{2,1,0:T(8,128)S(1)}, f32[1,48,128]{2,1,0:T(8,128)S(1)}, u32[]{:S(2)}, u32[]{:S(2)}) collective-permute-start(f32[1,48,128]{2,1,0:T(8,128)S(1)} %get-tuple-element.20), channel_id=1, source_target_pairs={{0,12},{2,14},{4,8},{6,10},{8,4},{10,6},{12,0},{14,2},{16,28},{18,... | collective-permute-start | bytes 73736 | tf_op jit(solution)/shard_map/ppermute | solution.py:264
  24.9 0.3 %collective-permute-start.5 = (f32[1,48,128]{2,1,0:T(8,128)S(1)}, f32[1,48,128]{2,1,0:T(8,128)S(1)}, u32[]{:S(2)}, u32[]{:S(2)}) collective-permute-start(f32[1,48,128]{2,1,0:T(8,128)S(1)} %get-tuple-element.19), channel_id=1, source_target_pairs={{0,8},{2,10},{4,12},{6,14},{8,0},{10,2},{12,4},{14,6},{16,24},{18,... | collective-permute-start | bytes 73736 | tf_op jit(solution)/shard_map/ppermute | solution.py:264
  25.3 1.9 %collective-permute-start.6 = (f32[1,48,128]{2,1,0:T(8,128)S(1)}, f32[1,48,128]{2,1,0:T(8,128)S(1)}, u32[]{:S(2)}, u32[]{:S(2)}) collective-permute-start(f32[1,48,128]{2,1,0:T(8,128)S(1)} %get-tuple-element.18), channel_id=1, source_target_pairs={{0,4},{2,6},{4,0},{6,2},{8,12},{10,14},{12,8},{14,10},{16,20},{18,... | collective-permute-start | bytes 73736 | tf_op jit(solution)/shard_map/ppermute | solution.py:264
  27.1 1.0 %collective-permute-done.7 = f32[4,24,128]{2,1,0:T(8,128)S(1)} collective-permute-done((f32[4,24,128]{2,1,0:T(8,128)S(1)}, f32[4,24,128]{2,1,0:T(8,128)S(1)}, u32[]{:S(2)}, u32[]{:S(2)}) %collective-permute-start.7) | collective-permute-done | bytes 49184 | tf_op jit(solution)/shard_map/last_hop/ppermute | solution.py:264
  28.1 0.4 %correction_body.1.refs_3_ = f32[3,2,8,128]{3,2,1,0:T(8,128)S(1)} custom-call(f32[8,24,128]{2,1,0:T(8,128)S(1)} %pad_maximum_fusion.cross_ref, f32[3,2,32,8]{3,2,1,0:T(8,128)S(1)} %solve_body.1.solved_ref), custom_call_target="tpu_custom_call" | custom-call | flops 100000000 | bytes 2000000 | tf_op jit(solution)/shard_map/correction_body/pallas_call | solution.py:273
  28.6 0.2 collective-permute-done.5.refs_0_
  28.8 0.3 %collective-permute-done.6.refs_1_ = f32[1,48,128]{2,1,0:T(8,128)S(1)} collective-permute-done((f32[1,48,128]{2,1,0:T(8,128)S(1)}, f32[1,48,128]{2,1,0:T(8,128)S(1)}, u32[]{:S(2)}, u32[]{:S(2)}) %collective-permute-start.6) | collective-permute-done | bytes 24608 | tf_op jit(solution)/shard_map/ppermute | solution.py:264
  29.1 0.6 %finish_body.1 = f32[3,2,8,128]{3,2,1,0:T(8,128)} custom-call(f32[1,48,128]{2,1,0:T(8,128)S(1)} %collective-permute-done.4.kept_ref, f32[1,48,128]{2,1,0:T(8,128)S(1)} %collective-permute-done.5.refs_0_, f32[1,48,128]{2,1,0:T(8,128)S(1)} %collective-permute-done.6.refs_1_, f32[1,48,128]{2,1,0:T(8,128)S(1)} %get-tuple-element.17.refs_2_, ...), custom_call_target="tpu_custom_call" | custom-call | tf_op jit(solution)/shard_map/finish_body/pallas_call | solution.py:273
  (17 shorter events, 0.2 us)
Async XLA Ops:
  0.0 0.9 %copy-start.1 = (bf16[3,2,8,2048]{3,2,1,0:T(8,128)(2,1)S(1)}, bf16[3,2,8,2048]{3,2,1,0:T(8,128)(2,1)}, u32[]{:S(2)}) copy-start(bf16[3,2,8,2048]{3,2,1,0:T(8,128)(2,1)} %volts_ref.5) | copy-start | bytes 589828
  0.9 8.3 %copy-start = (bf16[3,2,32,2048]{3,2,1,0:T(8,128)(2,1)S(1)}, bf16[3,2,32,2048]{3,2,1,0:T(8,128)(2,1)}, u32[]{:S(2)}) copy-start(bf16[3,2,32,2048]{3,2,1,0:T(8,128)(2,1)} %reference_ref.3) | copy-start | bytes 2359300
  1.7 7.5 %copy-start.2 = (bf16[3,2,8,2048]{3,2,1,0:T(8,128)(2,1)S(1)}, bf16[3,2,8,2048]{3,2,1,0:T(8,128)(2,1)}, u32[]{:S(2)}) copy-start(bf16[3,2,8,2048]{3,2,1,0:T(8,128)(2,1)} %volts_ref.5) | copy-start | bytes 589828
  1.7 20.1 %all-to-all-start = ((bf16[16,96,128]{2,1,0:T(8,128)(2,1)}), bf16[16,96,128]{2,1,0:T(8,128)(2,1)S(1)}, u32[]{:S(2)}, u32[]{:S(2)}) async-start(bf16[16,96,128]{2,1,0:T(8,128)(2,1)} %pack_body.1), calls=%async_computation | async-start | bytes 786432 | tf_op jit(solution)/shard_map/all_to_all | solution.py:297
  9.8 1.2 %collective-permute-start = (f32[1,16,128]{2,1,0:T(8,128)S(1)}, f32[1,16,128]{2,1,0:T(8,128)S(1)}, u32[]{:S(2)}, u32[]{:S(2)}) collective-permute-start(f32[1,16,128]{2,1,0:T(8,128)S(1)} %cross_body.1), channel_id=1, source_target_pairs={{0,2},{2,0},{4,6},{6,4},{8,10},{10,8},{12,14},{14,12},{16,18},{18,... | collective-permute-start | bytes 24584 | tf_op jit(solution)/shard_map/hop/ppermute | solution.py:264
  11.2 4.0 %collective-permute-start.1 = (f32[1,24,128]{2,1,0:T(8,128)S(1)}, f32[1,24,128]{2,1,0:T(8,128)S(1)}, u32[]{:S(2)}, u32[]{:S(2)}) collective-permute-start(f32[1,24,128]{2,1,0:T(8,128)S(1)} %maximum_maximum_fusion), channel_id=1, source_target_pairs={{0,4},{2,6},{4,0},{6,2},{8,12},{10,14},{12,8},{14,10},{16,20},{18,... | collective-permute-start | bytes 36872 | tf_op jit(solution)/shard_map/hop/ppermute | solution.py:264
  15.3 4.0 %collective-permute-start.2 = (f32[2,24,128]{2,1,0:T(8,128)S(1)}, f32[2,24,128]{2,1,0:T(8,128)S(1)}, u32[]{:S(2)}, u32[]{:S(2)}) collective-permute-start(f32[2,24,128]{2,1,0:T(8,128)S(1)} %pad_maximum_fusion.2), channel_id=1, source_target_pairs={{0,8},{2,10},{4,12},{6,14},{8,0},{10,2},{12,4},{14,6},{16,24},{18,... | collective-permute-start | bytes 73736 | tf_op jit(solution)/shard_map/hop/ppermute | solution.py:264
  22.0 1.5 %collective-permute-start.3 = (f32[4,48,128]{2,1,0:T(8,128)S(1)}, f32[4,48,128]{2,1,0:T(8,128)S(1)}, u32[]{:S(2)}, u32[]{:S(2)}) collective-permute-start(f32[4,48,128]{2,1,0:T(8,128)S(1)} %get-tuple-element.14), channel_id=1, source_target_pairs={{0,2},{2,0},{4,6},{6,4},{8,10},{10,8},{12,14},{14,12},{16,18},{18,... | collective-permute-start | bytes 294920 | tf_op jit(solution)/shard_map/ppermute | solution.py:264
  22.1 6.0 %collective-permute-start.7 = (f32[4,24,128]{2,1,0:T(8,128)S(1)}, f32[4,24,128]{2,1,0:T(8,128)S(1)}, u32[]{:S(2)}, u32[]{:S(2)}) collective-permute-start(f32[4,24,128]{2,1,0:T(8,128)S(1)} %pad_maximum_fusion.1), channel_id=1, source_target_pairs={{0,16},{2,18},{4,20},{6,22},{8,24},{10,26},{12,28},{14,30},{16,0},... | collective-permute-start | bytes 147464 | tf_op jit(solution)/shard_map/last_hop/ppermute | solution.py:264
  23.6 5.0 %collective-permute-start.4 = (f32[1,48,128]{2,1,0:T(8,128)S(1)}, f32[1,48,128]{2,1,0:T(8,128)S(1)}, u32[]{:S(2)}, u32[]{:S(2)}) collective-permute-start(f32[1,48,128]{2,1,0:T(8,128)S(1)} %get-tuple-element.20), channel_id=1, source_target_pairs={{0,12},{2,14},{4,8},{6,10},{8,4},{10,6},{12,0},{14,2},{16,28},{18,... | collective-permute-start | bytes 73736 | tf_op jit(solution)/shard_map/ppermute | solution.py:264
  24.9 3.8 %collective-permute-start.5 = (f32[1,48,128]{2,1,0:T(8,128)S(1)}, f32[1,48,128]{2,1,0:T(8,128)S(1)}, u32[]{:S(2)}, u32[]{:S(2)}) collective-permute-start(f32[1,48,128]{2,1,0:T(8,128)S(1)} %get-tuple-element.19), channel_id=1, source_target_pairs={{0,8},{2,10},{4,12},{6,14},{8,0},{10,2},{12,4},{14,6},{16,24},{18,... | collective-permute-start | bytes 73736 | tf_op jit(solution)/shard_map/ppermute | solution.py:264
  25.3 3.8 %collective-permute-start.6 = (f32[1,48,128]{2,1,0:T(8,128)S(1)}, f32[1,48,128]{2,1,0:T(8,128)S(1)}, u32[]{:S(2)}, u32[]{:S(2)}) collective-permute-start(f32[1,48,128]{2,1,0:T(8,128)S(1)} %get-tuple-element.18), channel_id=1, source_target_pairs={{0,4},{2,6},{4,0},{6,2},{8,12},{10,14},{12,8},{14,10},{16,20},{18,... | collective-permute-start | bytes 73736 | tf_op jit(solution)/shard_map/ppermute | solution.py:264

commit v6 on v5

--- a/solution.py
+++ b/solution.py
@@ -123,13 +123,13 @@
         second = jnp.concatenate([ref_imag, imag], 0)
         reals.append((dot(ref_real, first) + dot(ref_imag, second)) / jnp.float32(samples))
         imags.append((dot(ref_imag, first) - dot(ref_real, second)) / jnp.float32(samples))
-    re, im = eliminate(jnp.stack(reals), jnp.stack(imags), 0, nref // 2)
+    re, im = eliminate(jnp.stack(reals), jnp.stack(imags), 0, 3 * nref // 8)
     system_ref[0], system_ref[1] = re, im
 
 
 def solve_body(system_ref, solved_ref):
     nref = system_ref.shape[2]
-    re, im = eliminate(system_ref[0], system_ref[1], nref // 2, nref)
+    re, im = eliminate(system_ref[0], system_ref[1], 3 * nref // 8, nref)
     solved_ref[:, 0] = re[:, :, nref:]
     solved_ref[:, 1] = im[:, :, nref:]
 

time: 29.9 us -> 29.9 us (level)
  transfers between devices with their start and end apart: 9 -> 9, of which waited for: 6 -> 7; matrix products, arithmetic and copies ran while one was open for 1% -> 1% of each run, Pallas kernels for 16% -> 16%
where the time goes in v6:
time: 29.9 us; the launch traced here: 29.7 us
  starting transfers between devices  16.5 us (55%)
  Pallas kernels  6.4 us (21%)
  waiting for transfers between devices  5.56 us (19%)
  local copies, waits for them, and re-layouts  0.95 us (3%)
    ppermute x8, starting transfers between devices, swap(): return lax.ppermute(x, 'row', [(i, i ^ bit) for i in range(n_row)])  8.95 us
    all_to_all x1, starting transfers between devices, per_device(): lax.all_to_all(message, 'row', split_axis=0, concat_axis=0, tiled=True)  7.52 us
    pallas_call x7, Pallas kernels, call(): pl.pallas_call(functools.partial(body, **kw) if kw else body, out_shape=o...  6.4 us
    ppermute x8, waiting for transfers between devices, swap(): return lax.ppermute(x, 'row', [(i, i ^ bit) for i in range(n_row)])  3.07 us
    all_to_all x1, waiting for transfers between devices, per_device(): lax.all_to_all(message, 'row', split_axis=0, concat_axis=0, tiled=True)  2.49 us
    unnamed x6, local copies, waits for them, and re-layouts  0.93 us
  transfers between devices with their start and end apart: 9, of which 7 were waited for; matrix products, arithmetic and copies ran while one was open for 1% of the time, Pallas kernels for 16%

profile of v6, /device:TPU:0, one launch (start us, length us, event | category | flops | bytes accessed | tf_op | source)
XLA Modules:
  0.0 29.7 jit_solution(10709957993343869251)
XLA Ops:
  0.0 0.9 %copy-done.1 = bf16[3,2,8,2048]{3,2,1,0:T(8,128)(2,1)S(1)} copy-done((bf16[3,2,8,2048]{3,2,1,0:T(8,128)(2,1)S(1)}, bf16[3,2,8,2048]{3,2,1,0:T(8,128)(2,1)}, u32[]{:S(2)}) %copy-start.1) | copy-done | bytes 196632
  0.9 0.8 %pack_body.1 = bf16[16,96,128]{2,1,0:T(8,128)(2,1)} custom-call(bf16[3,2,8,2048]{3,2,1,0:T(8,128)(2,1)S(1)} %copy-done.1), custom_call_target="tpu_custom_call" | custom-call | tf_op jit(solution)/shard_map/pack_body/pallas_call | solution.py:273
  1.7 7.5 %all-to-all-start = ((bf16[16,96,128]{2,1,0:T(8,128)(2,1)}), bf16[16,96,128]{2,1,0:T(8,128)(2,1)S(1)}, u32[]{:S(2)}, u32[]{:S(2)}) async-start(bf16[16,96,128]{2,1,0:T(8,128)(2,1)} %pack_body.1), calls=%async_computation | async-start | bytes 786432 | tf_op jit(solution)/shard_map/all_to_all | solution.py:297
  9.3 0.6 %cross_body.1 = f32[1,16,128]{2,1,0:T(8,128)S(1)} custom-call(bf16[3,2,8,2048]{3,2,1,0:T(8,128)(2,1)S(1)} %copy-done.2, bf16[3,2,32,2048]{3,2,1,0:T(8,128)(2,1)S(1)} %copy-done), custom_call_target="tpu_custom_call" | custom-call | flops 100000000 | bytes 1000000 | tf_op jit(solution)/shard_map/cross_body/pallas_call | solution.py:273
  9.8 0.4 %collective-permute-start = (f32[1,16,128]{2,1,0:T(8,128)S(1)}, f32[1,16,128]{2,1,0:T(8,128)S(1)}, u32[]{:S(2)}, u32[]{:S(2)}) collective-permute-start(f32[1,16,128]{2,1,0:T(8,128)S(1)} %cross_body.1), channel_id=1, source_target_pairs={{0,2},{2,0},{4,6},{6,4},{8,10},{10,8},{12,14},{14,12},{16,18},{18,... | collective-permute-start | bytes 24584 | tf_op jit(solution)/shard_map/hop/ppermute | solution.py:264
  10.3 0.8 %collective-permute-done = f32[1,16,128]{2,1,0:T(8,128)S(1)} collective-permute-done((f32[1,16,128]{2,1,0:T(8,128)S(1)}, f32[1,16,128]{2,1,0:T(8,128)S(1)}, u32[]{:S(2)}, u32[]{:S(2)}) %collective-permute-start) | collective-permute-done | bytes 8224 | tf_op jit(solution)/shard_map/hop/ppermute | solution.py:264
  11.1 0.1 maximum_maximum_fusion
  11.2 1.9 %collective-permute-start.1 = (f32[1,24,128]{2,1,0:T(8,128)S(1)}, f32[1,24,128]{2,1,0:T(8,128)S(1)}, u32[]{:S(2)}, u32[]{:S(2)}) collective-permute-start(f32[1,24,128]{2,1,0:T(8,128)S(1)} %maximum_maximum_fusion), channel_id=1, source_target_pairs={{0,4},{2,6},{4,0},{6,2},{8,12},{10,14},{12,8},{14,10},{16,20},{18,... | collective-permute-start | bytes 36872 | tf_op jit(solution)/shard_map/hop/ppermute | solution.py:264
  13.0 1.7 %system_body.1.system_ref = f32[2,3,32,40]{3,2,1,0:T(8,128)S(1)} custom-call(bf16[3,2,8,2048]{3,2,1,0:T(8,128)(2,1)S(1)} %copy-done.2, bf16[3,2,32,2048]{3,2,1,0:T(8,128)(2,1)S(1)} %copy-done), custom_call_target="tpu_custom_call" | custom-call | flops 1000000000 | bytes 20000000 | tf_op jit(solution)/shard_map/system_body/pallas_call | solution.py:273
  14.8 0.3 %collective-permute-done.1 = f32[1,24,128]{2,1,0:T(8,128)S(1)} collective-permute-done((f32[1,24,128]{2,1,0:T(8,128)S(1)}, f32[1,24,128]{2,1,0:T(8,128)S(1)}, u32[]{:S(2)}, u32[]{:S(2)}) %collective-permute-start.1) | collective-permute-done | bytes 12320 | tf_op jit(solution)/shard_map/hop/ppermute | solution.py:264
  15.2 1.6 %collective-permute-start.2 = (f32[2,24,128]{2,1,0:T(8,128)S(1)}, f32[2,24,128]{2,1,0:T(8,128)S(1)}, u32[]{:S(2)}, u32[]{:S(2)}) collective-permute-start(f32[2,24,128]{2,1,0:T(8,128)S(1)} %pad_maximum_fusion.2), channel_id=1, source_target_pairs={{0,8},{2,10},{4,12},{6,14},{8,0},{10,2},{12,4},{14,6},{16,24},{18,... | collective-permute-start | bytes 73736 | tf_op jit(solution)/shard_map/hop/ppermute | solution.py:264
  16.8 2.0 %solve_body.1.solved_ref = f32[3,2,32,8]{3,2,1,0:T(8,128)S(1)} custom-call(f32[2,3,32,40]{3,2,1,0:T(8,128)S(1)} %system_body.1.system_ref), custom_call_target="tpu_custom_call" | custom-call | flops 1000000000 | bytes 20000000 | tf_op jit(solution)/shard_map/solve_body/pallas_call | solution.py:273
  18.8 0.4 %collective-permute-done.2 = f32[2,24,128]{2,1,0:T(8,128)S(1)} collective-permute-done((f32[2,24,128]{2,1,0:T(8,128)S(1)}, f32[2,24,128]{2,1,0:T(8,128)S(1)}, u32[]{:S(2)}, u32[]{:S(2)}) %collective-permute-start.2) | collective-permute-done | bytes 24608 | tf_op jit(solution)/shard_map/hop/ppermute | solution.py:264
  19.3 2.5 %all-to-all-done.message_ref = bf16[16,96,128]{2,1,0:T(8,128)(2,1)S(1)} async-done(((bf16[16,96,128]{2,1,0:T(8,128)(2,1)}), bf16[16,96,128]{2,1,0:T(8,128)(2,1)S(1)}, u32[]{:S(2)}, u32[]{:S(2)}) %all-to-all-start) | async-done | bytes 393248 | tf_op jit(solution)/shard_map/all_to_all | solution.py:297
  21.8 0.3 product_body.1
  22.1 1.4 %collective-permute-start.7 = (f32[4,24,128]{2,1,0:T(8,128)S(1)}, f32[4,24,128]{2,1,0:T(8,128)S(1)}, u32[]{:S(2)}, u32[]{:S(2)}) collective-permute-start(f32[4,24,128]{2,1,0:T(8,128)S(1)} %pad_maximum_fusion.1), channel_id=1, source_target_pairs={{0,16},{2,18},{4,20},{6,22},{8,24},{10,26},{12,28},{14,30},{16,0},... | collective-permute-start | bytes 147464 | tf_op jit(solution)/shard_map/last_hop/ppermute | solution.py:264
  23.6 1.4 %collective-permute-start.4 = (f32[1,48,128]{2,1,0:T(8,128)S(1)}, f32[1,48,128]{2,1,0:T(8,128)S(1)}, u32[]{:S(2)}, u32[]{:S(2)}) collective-permute-start(f32[1,48,128]{2,1,0:T(8,128)S(1)} %get-tuple-element.20), channel_id=1, source_target_pairs={{0,12},{2,14},{4,8},{6,10},{8,4},{10,6},{12,0},{14,2},{16,28},{18,... | collective-permute-start | bytes 73736 | tf_op jit(solution)/shard_map/ppermute | solution.py:264
  24.9 0.3 %collective-permute-start.5 = (f32[1,48,128]{2,1,0:T(8,128)S(1)}, f32[1,48,128]{2,1,0:T(8,128)S(1)}, u32[]{:S(2)}, u32[]{:S(2)}) collective-permute-start(f32[1,48,128]{2,1,0:T(8,128)S(1)} %get-tuple-element.19), channel_id=1, source_target_pairs={{0,8},{2,10},{4,12},{6,14},{8,0},{10,2},{12,4},{14,6},{16,24},{18,... | collective-permute-start | bytes 73736 | tf_op jit(solution)/shard_map/ppermute | solution.py:264
  25.3 1.9 %collective-permute-start.6 = (f32[1,48,128]{2,1,0:T(8,128)S(1)}, f32[1,48,128]{2,1,0:T(8,128)S(1)}, u32[]{:S(2)}, u32[]{:S(2)}) collective-permute-start(f32[1,48,128]{2,1,0:T(8,128)S(1)} %get-tuple-element.18), channel_id=1, source_target_pairs={{0,4},{2,6},{4,0},{6,2},{8,12},{10,14},{12,8},{14,10},{16,20},{18,... | collective-permute-start | bytes 73736 | tf_op jit(solution)/shard_map/ppermute | solution.py:264
  27.1 1.0 %collective-permute-done.7 = f32[4,24,128]{2,1,0:T(8,128)S(1)} collective-permute-done((f32[4,24,128]{2,1,0:T(8,128)S(1)}, f32[4,24,128]{2,1,0:T(8,128)S(1)}, u32[]{:S(2)}, u32[]{:S(2)}) %collective-permute-start.7) | collective-permute-done | bytes 49184 | tf_op jit(solution)/shard_map/last_hop/ppermute | solution.py:264
  28.1 0.4 %correction_body.1.refs_3_ = f32[3,2,8,128]{3,2,1,0:T(8,128)S(1)} custom-call(f32[8,24,128]{2,1,0:T(8,128)S(1)} %pad_maximum_fusion.cross_ref, f32[3,2,32,8]{3,2,1,0:T(8,128)S(1)} %solve_body.1.solved_ref), custom_call_target="tpu_custom_call" | custom-call | flops 100000000 | bytes 2000000 | tf_op jit(solution)/shard_map/correction_body/pallas_call | solution.py:273
  28.6 0.2 collective-permute-done.5.refs_0_
  28.8 0.3 %collective-permute-done.6.refs_1_ = f32[1,48,128]{2,1,0:T(8,128)S(1)} collective-permute-done((f32[1,48,128]{2,1,0:T(8,128)S(1)}, f32[1,48,128]{2,1,0:T(8,128)S(1)}, u32[]{:S(2)}, u32[]{:S(2)}) %collective-permute-start.6) | collective-permute-done | bytes 24608 | tf_op jit(solution)/shard_map/ppermute | solution.py:264
  29.1 0.6 %finish_body.1 = f32[3,2,8,128]{3,2,1,0:T(8,128)} custom-call(f32[1,48,128]{2,1,0:T(8,128)S(1)} %collective-permute-done.4.kept_ref, f32[1,48,128]{2,1,0:T(8,128)S(1)} %collective-permute-done.5.refs_0_, f32[1,48,128]{2,1,0:T(8,128)S(1)} %collective-permute-done.6.refs_1_, f32[1,48,128]{2,1,0:T(8,128)S(1)} %get-tuple-element.17.refs_2_, ...), custom_call_target="tpu_custom_call" | custom-call | tf_op jit(solution)/shard_map/finish_body/pallas_call | solution.py:273
  (17 shorter events, 0.3 us)
Async XLA Ops:
  0.0 0.9 %copy-start.1 = (bf16[3,2,8,2048]{3,2,1,0:T(8,128)(2,1)S(1)}, bf16[3,2,8,2048]{3,2,1,0:T(8,128)(2,1)}, u32[]{:S(2)}) copy-start(bf16[3,2,8,2048]{3,2,1,0:T(8,128)(2,1)} %volts_ref.5) | copy-start | bytes 589828
  0.9 8.3 %copy-start = (bf16[3,2,32,2048]{3,2,1,0:T(8,128)(2,1)S(1)}, bf16[3,2,32,2048]{3,2,1,0:T(8,128)(2,1)}, u32[]{:S(2)}) copy-start(bf16[3,2,32,2048]{3,2,1,0:T(8,128)(2,1)} %reference_ref.3) | copy-start | bytes 2359300
  1.7 7.5 %copy-start.2 = (bf16[3,2,8,2048]{3,2,1,0:T(8,128)(2,1)S(1)}, bf16[3,2,8,2048]{3,2,1,0:T(8,128)(2,1)}, u32[]{:S(2)}) copy-start(bf16[3,2,8,2048]{3,2,1,0:T(8,128)(2,1)} %volts_ref.5) | copy-start | bytes 589828
  1.7 20.1 %all-to-all-start = ((bf16[16,96,128]{2,1,0:T(8,128)(2,1)}), bf16[16,96,128]{2,1,0:T(8,128)(2,1)S(1)}, u32[]{:S(2)}, u32[]{:S(2)}) async-start(bf16[16,96,128]{2,1,0:T(8,128)(2,1)} %pack_body.1), calls=%async_computation | async-start | bytes 786432 | tf_op jit(solution)/shard_map/all_to_all | solution.py:297
  9.8 1.2 %collective-permute-start = (f32[1,16,128]{2,1,0:T(8,128)S(1)}, f32[1,16,128]{2,1,0:T(8,128)S(1)}, u32[]{:S(2)}, u32[]{:S(2)}) collective-permute-start(f32[1,16,128]{2,1,0:T(8,128)S(1)} %cross_body.1), channel_id=1, source_target_pairs={{0,2},{2,0},{4,6},{6,4},{8,10},{10,8},{12,14},{14,12},{16,18},{18,... | collective-permute-start | bytes 24584 | tf_op jit(solution)/shard_map/hop/ppermute | solution.py:264
  11.2 3.9 %collective-permute-start.1 = (f32[1,24,128]{2,1,0:T(8,128)S(1)}, f32[1,24,128]{2,1,0:T(8,128)S(1)}, u32[]{:S(2)}, u32[]{:S(2)}) collective-permute-start(f32[1,24,128]{2,1,0:T(8,128)S(1)} %maximum_maximum_fusion), channel_id=1, source_target_pairs={{0,4},{2,6},{4,0},{6,2},{8,12},{10,14},{12,8},{14,10},{16,20},{18,... | collective-permute-start | bytes 36872 | tf_op jit(solution)/shard_map/hop/ppermute | solution.py:264
  15.2 4.0 %collective-permute-start.2 = (f32[2,24,128]{2,1,0:T(8,128)S(1)}, f32[2,24,128]{2,1,0:T(8,128)S(1)}, u32[]{:S(2)}, u32[]{:S(2)}) collective-permute-start(f32[2,24,128]{2,1,0:T(8,128)S(1)} %pad_maximum_fusion.2), channel_id=1, source_target_pairs={{0,8},{2,10},{4,12},{6,14},{8,0},{10,2},{12,4},{14,6},{16,24},{18,... | collective-permute-start | bytes 73736 | tf_op jit(solution)/shard_map/hop/ppermute | solution.py:264
  22.0 1.5 %collective-permute-start.3 = (f32[4,48,128]{2,1,0:T(8,128)S(1)}, f32[4,48,128]{2,1,0:T(8,128)S(1)}, u32[]{:S(2)}, u32[]{:S(2)}) collective-permute-start(f32[4,48,128]{2,1,0:T(8,128)S(1)} %get-tuple-element.14), channel_id=1, source_target_pairs={{0,2},{2,0},{4,6},{6,4},{8,10},{10,8},{12,14},{14,12},{16,18},{18,... | collective-permute-start | bytes 294920 | tf_op jit(solution)/shard_map/ppermute | solution.py:264
  22.1 6.0 %collective-permute-start.7 = (f32[4,24,128]{2,1,0:T(8,128)S(1)}, f32[4,24,128]{2,1,0:T(8,128)S(1)}, u32[]{:S(2)}, u32[]{:S(2)}) collective-permute-start(f32[4,24,128]{2,1,0:T(8,128)S(1)} %pad_maximum_fusion.1), channel_id=1, source_target_pairs={{0,16},{2,18},{4,20},{6,22},{8,24},{10,26},{12,28},{14,30},{16,0},... | collective-permute-start | bytes 147464 | tf_op jit(solution)/shard_map/last_hop/ppermute | solution.py:264
  23.6 5.0 %collective-permute-start.4 = (f32[1,48,128]{2,1,0:T(8,128)S(1)}, f32[1,48,128]{2,1,0:T(8,128)S(1)}, u32[]{:S(2)}, u32[]{:S(2)}) collective-permute-start(f32[1,48,128]{2,1,0:T(8,128)S(1)} %get-tuple-element.20), channel_id=1, source_target_pairs={{0,12},{2,14},{4,8},{6,10},{8,4},{10,6},{12,0},{14,2},{16,28},{18,... | collective-permute-start | bytes 73736 | tf_op jit(solution)/shard_map/ppermute | solution.py:264
  24.9 3.8 %collective-permute-start.5 = (f32[1,48,128]{2,1,0:T(8,128)S(1)}, f32[1,48,128]{2,1,0:T(8,128)S(1)}, u32[]{:S(2)}, u32[]{:S(2)}) collective-permute-start(f32[1,48,128]{2,1,0:T(8,128)S(1)} %get-tuple-element.19), channel_id=1, source_target_pairs={{0,8},{2,10},{4,12},{6,14},{8,0},{10,2},{12,4},{14,6},{16,24},{18,... | collective-permute-start | bytes 73736 | tf_op jit(solution)/shard_map/ppermute | solution.py:264
  25.3 3.8 %collective-permute-start.6 = (f32[1,48,128]{2,1,0:T(8,128)S(1)}, f32[1,48,128]{2,1,0:T(8,128)S(1)}, u32[]{:S(2)}, u32[]{:S(2)}) collective-permute-start(f32[1,48,128]{2,1,0:T(8,128)S(1)} %get-tuple-element.18), channel_id=1, source_target_pairs={{0,4},{2,6},{4,0},{6,2},{8,12},{10,14},{12,8},{14,10},{16,20},{18,... | collective-permute-start | bytes 73736 | tf_op jit(solution)/shard_map/ppermute | solution.py:264
